TPU v7x, 256 devices: a whole 4x4x8 slice. The times are simulated.
256 devices in a mesh: freq: 32 (over y, x, core), tile: 8 (over z).
Axes of the slice: x: 4, y: 4, z: 8, core: 2. Of those that a mesh axis runs over, the one named last changes fastest.
Arguments:
- left_factor: bfloat16 [128, 16, 32, 2, 16, 256], P('freq', 'tile'), may hold values from -1.5 to 1.5
- right_factor: bfloat16 [128, 16, 32, 2, 16, 256], P('freq', None, 'tile'), may hold values from -0.0625 to 0.0625
- tile_ranks: int32 [128, 16, 32], P('freq'), may hold values from 1 to 16
- tile_scales: float32 [128, 2, 16, 32], P('freq'), may hold values from 0.5 to 2
- recorded: float32 [128, 2, 8, 4096], P('freq', None, None, 'tile'), may hold values from -12 to 12
- step_sizes: float32 [128], P('freq'), may hold values from 0.2 to 0.6
- thresholds: float32 [8], replicated, may hold values from 0.1 to 0.5
Outputs:
- estimate: float32 [128, 2, 8, 8192], P('freq', None, None, 'tile')
Inputs may be any that keep to these rules, and one draw needn't show every extreme that they name: `tile_ranks`: rank of each tile; rank slots at and above it carry no weight.
All inputs are finite; a program needn't handle non-finite values.
Results may differ from a plain program's by a relative error of at most 0.0058.
Values may be sent and summed in bfloat16 or wider, within the bound.
No kernel may reach another device: no remote copies, remote signals or barrier semaphores. Data moves between devices by JAX's collectives and lax.ppermute only.
A program may use at most 128 MiB of HBM per device.

v0:
```python
import math

import jax
import jax.numpy as jnp
from jax import lax
from jax.sharding import PartitionSpec as P

F = 128


def dft_tables(freq_index, time_count):
    times_row = jnp.arange(time_count, dtype=jnp.int32)
    phase_steps = (freq_index[:, None] * times_row[None, :] % time_count).astype(jnp.float32)
    angles = phase_steps * (2.0 * math.pi / time_count)
    scaling = jnp.where(
        freq_index == 0, math.sqrt(1.0 / time_count), math.sqrt(2.0 / time_count)
    ).astype(jnp.float32)
    return (scaling[:, None] * jnp.cos(angles), scaling[:, None] * jnp.sin(angles))


def slot_weights(tile_ranks, tile_scales, rank_max):
    slot_index = jnp.arange(rank_max, dtype=jnp.int32)
    live_slots = (slot_index < tile_ranks[..., None]).astype(jnp.float32)
    return (tile_scales[:, 0] * tile_scales[:, 1])[..., None] * live_slots


def per_device(
    left_factor, right_factor, tile_ranks, tile_scales, recorded, step_sizes, thresholds
):
    freqs_here = left_factor.shape[0]
    rows_here = left_factor.shape[1]
    col_tiles = left_factor.shape[2]
    rank_max = left_factor.shape[4]
    tile_width = left_factor.shape[5]
    row_tiles = right_factor.shape[1]
    cols_here = right_factor.shape[2]
    virtual = recorded.shape[2]
    tile_pos = lax.axis_index("tile")
    freq_pos = lax.axis_index("freq")
    columns_here = cols_here * tile_width
    time_count = 2 * F
    highest = lax.Precision.HIGHEST
    weights = slot_weights(tile_ranks, tile_scales, rank_max)
    weights_right = lax.dynamic_slice_in_dim(weights, tile_pos * cols_here, cols_here, 2)
    weights_left = lax.dynamic_slice_in_dim(weights, tile_pos * rows_here, rows_here, 1)
    left_real = left_factor[:, :, :, 0]
    left_imag = left_factor[:, :, :, 1]
    right_real = right_factor[:, :, :, 0]
    right_imag = right_factor[:, :, :, 1]
    cos_all, sin_all = dft_tables(jnp.arange(F, dtype=jnp.int32), time_count)

    def gradient(residual):
        halves = residual.astype(jnp.bfloat16).reshape(
            freqs_here, 2, virtual, rows_here, tile_width
        )

        def contract_left(matrix, vectors):
            return jnp.einsum(
                "fijkq,fviq->fijkv", matrix, vectors, preferred_element_type=jnp.float32
            )

        dual_real = contract_left(left_real, halves[:, 0]) + contract_left(left_imag, halves[:, 1])
        dual_imag = contract_left(left_real, halves[:, 1]) - contract_left(left_imag, halves[:, 0])
        duals = (
            jnp.stack([dual_real, dual_imag], 3) * weights_left[:, :, :, None, :, None]
        ).astype(jnp.bfloat16)
        duals = duals.reshape(freqs_here, rows_here, col_tiles, 2, rank_max * virtual)
        arrived = lax.all_to_all(duals, "tile", split_axis=2, concat_axis=1, tiled=True)
        arrived = arrived.reshape(freqs_here, row_tiles, cols_here, 2, rank_max, virtual)

        def spread(matrix, vectors):
            return jnp.einsum(
                "fijkp,fijkv->fvjp", matrix, vectors, preferred_element_type=jnp.float32
            )

        grad_real = spread(right_real, arrived[:, :, :, 0]) - spread(
            right_imag, arrived[:, :, :, 1]
        )
        grad_imag = spread(right_real, arrived[:, :, :, 1]) + spread(
            right_imag, arrived[:, :, :, 0]
        )
        return jnp.stack([grad_real, grad_imag], 1).reshape(freqs_here, 2, virtual, columns_here)

    def to_time(wavefield):
        own_freqs = freq_pos * freqs_here + jnp.arange(freqs_here, dtype=jnp.int32)
        cos_own, sin_own = dft_tables(own_freqs, time_count)
        return lax.psum_scatter(
            jnp.einsum("fvn,ft->nvt", wavefield[:, 0], cos_own, precision=highest)
            - jnp.einsum("fvn,ft->nvt", wavefield[:, 1], sin_own, precision=highest),
            "freq",
            scatter_dimension=0,
            tiled=True,
        )

    def shrink(signal):
        excess = jnp.abs(signal) - thresholds[None, :, None]
        return jnp.sign(signal) * jnp.maximum(excess, 0.0)

    def to_freq(signal):
        real_part = jnp.einsum("nvt,ft->fvn", signal, cos_all, precision=highest)
        imag_part = -jnp.einsum("nvt,ft->fvn", signal, sin_all, precision=highest)
        return lax.all_to_all(
            jnp.stack([real_part, imag_part], 1), "freq", split_axis=0, concat_axis=3, tiled=True
        )

    scaled = step_sizes[:, None, None, None]
    first = to_freq(shrink(to_time(scaled * gradient(recorded))))
    halves = first.astype(jnp.bfloat16).reshape(freqs_here, 2, virtual, cols_here, tile_width)

    def project(matrix, vectors):
        return jnp.einsum("fijkp,fvjp->fijkv", matrix, vectors, preferred_element_type=jnp.float32)

    coef_real = project(right_real, halves[:, 0]) + project(right_imag, halves[:, 1])
    coef_imag = project(right_real, halves[:, 1]) - project(right_imag, halves[:, 0])
    coeffs = (jnp.stack([coef_real, coef_imag], 3) * weights_right[:, :, :, None, :, None]).astype(
        jnp.bfloat16
    )
    coeffs = coeffs.reshape(freqs_here, row_tiles, cols_here, 2, rank_max * virtual)
    arrived = lax.all_to_all(coeffs, "tile", split_axis=1, concat_axis=2, tiled=True)
    arrived = arrived.reshape(freqs_here, rows_here, col_tiles, 2, rank_max, virtual)

    def expand(matrix, vectors):
        return jnp.einsum("fijkq,fijkv->fviq", matrix, vectors, preferred_element_type=jnp.float32)

    image_real = expand(left_real, arrived[:, :, :, 0]) - expand(left_imag, arrived[:, :, :, 1])
    image_imag = expand(left_real, arrived[:, :, :, 1]) + expand(left_imag, arrived[:, :, :, 0])
    return to_freq(
        shrink(
            to_time(
                first
                + scaled
                * gradient(
                    recorded
                    - jnp.stack([image_real, image_imag], 1).reshape(
                        freqs_here, 2, virtual, rows_here * tile_width
                    )
                )
            )
        )
    )


def solution(mesh):
    return jax.shard_map(
        per_device,
        mesh=mesh,
        in_specs=(
            P("freq", "tile", None, None, None, None),
            P("freq", None, "tile", None, None, None),
            P("freq", None, None),
            P("freq", None, None, None),
            P("freq", None, None, "tile"),
            P("freq"),
            P(),
        ),
        out_specs=P("freq", None, None, "tile"),
        check_vma=False,
    )
```

profile of v0, /device:TPU:1, one launch (start us, length us, event | category | flops | bytes accessed | tf_op | source)
XLA Modules:
  0.0 459.0 jit_solution(16702514054860890911)
XLA Ops:
  9.5 4.3 fusion.99
  13.8 4.2 fusion.100
  18.0 3.6 convolution_add_fusion.1
  23.3 4.2 convolution_subtract_fusion.1
  28.9 9.0 %all-to-all-start = ((bf16[4,2,32,2,128]{4,0,3,1,2:T(4,128)(2,1)}), bf16[4,2,32,2,128]{4,0,3,1,2:T(4,128)(2,1)S(1)}, u32[]{:S(2)}, u32[]{:S(2)}) async-start(bf16[4,2,32,2,128]{4,0,3,1,2:T(4,128)(2,1)} %copy.380), calls=%async_computation | async-start | bytes 262144 | tf_op jit(solution)/shard_map/all_to_all | solution.py:68
  38.1 4.1 fusion.148
  42.2 3.4 all-to-all-done
  45.8 3.4 reshape.83
  49.1 3.3 fusion.151
  62.5 6.8 %fusion.82 = f32[256,8,1024]{2,0,1:T(8,128)S(1)} fusion(f32[4,2,8,1024]{3,0,2,1:T(4,128)S(1)} %maximum_multiply_fusion.2, s32[4]{0:T(128)S(1)} %iota_add_fusion, f32[4]{0:T(128)S(1)} %compare_select_fusion), kind=kOutput, calls=%fused_computation.103 | convolution fusion | flops 100678656 | bytes 8520704 | tf_op jit(solution)/shard_map/fvn,ft->nvt/dot_general | solution.py:88
  69.3 9.6 %subtract_bitcast_fusion.1 = f32[1024,8,256]{0,2,1:T(8,128)} fusion(f32[256,8,1024]{2,0,1:T(8,128)S(1)} %fusion.82, f32[4,2,8,1024]{3,0,2,1:T(4,128)S(1)} %maximum_multiply_fusion.2, s32[4]{0:T(128)S(1)} %iota_add_fusion, f32[4]{0:T(128)S(1)} %compare_select_fusion), kind=kOutput, calls=%fused_computation.1 | convolution fusion | flops 102775808 | bytes 16909312 | tf_op jit(solution)/shard_map/fvn,ft->nvt/dot_general | solution.py:89
  78.9 9.3 %copy.389 = f32[1024,8,256]{2,1,0:T(8,128)} copy(f32[1024,8,256]{0,2,1:T(8,128)} %subtract_bitcast_fusion.1) | data formatting | bytes 16777216 | tf_op jit(solution)/shard_map/sub | solution.py:88
  88.9 96.6 %reduce-scatter.3.cloned.1.call-done = f32[32,8,256]{2,1,0:T(8,128)} async-done(((f32[1024,8,256]{2,1,0:T(8,128)}), f32[32,8,256]{2,1,0:T(8,128)}) %reduce-scatter.3.cloned.1.call-update) | async-done | bytes 262160 | tf_op jit(solution)/shard_map/reduce_scatter | solution.py:87
  190.1 7.9 %all-to-all-start.1 = ((f32[32,1,2048]{2,1,0:T(1,128)}), f32[32,1,2048]{2,1,0:T(1,128)S(1)}, u32[]{:S(2)}, u32[]{:S(2)}) async-start(f32[32,1,2048]{2,1,0:T(1,128)} %reshape.109), calls=%async_computation.2 | async-start | bytes 524288 | tf_op jit(solution)/shard_map/all_to_all | solution.py:102
  200.0 6.8 %all-to-all-done.1 = f32[32,1,2048]{2,1,0:T(1,128)S(1)} async-done(((f32[32,1,2048]{2,1,0:T(1,128)}), f32[32,1,2048]{2,1,0:T(1,128)S(1)}, u32[]{:S(2)}, u32[]{:S(2)}) %all-to-all-start.1) | async-done | bytes 262176 | tf_op jit(solution)/shard_map/all_to_all | solution.py:102
  214.1 3.5 fusion.57
  217.7 3.6 fusion.1
  223.9 4.8 %fusion = f32[4,16,4,16,8]{3,4,1,2,0:T(8,128)} fusion(f32[4,4,8,16,16]{4,2,3,1,0:T(8,128)} %fusion.57, bf16[4,16,4,1,16,256]{5,4,3,2,1,0:T(8,128)(2,1)S(1)} %copy-done.5, bf16[4,1,8,4,256]{4,3,2,1,0:T(4,128)(2,1)S(1)} %get-tuple-element.15), kind=kOutput, calls=%fused_computation.8 | convolution fusion | flops 16809984 | bytes 2424832 | tf_op jit(solution)/shard_map/fijkp,fvjp->fijkv/dot_general | solution.py:111
  236.2 6.9 %all-to-all-start.2 = ((bf16[4,16,4,2,128]{4,2,3,0,1:T(4,128)(2,1)}), bf16[4,16,4,2,128]{4,2,3,0,1:T(4,128)(2,1)S(1)}, u32[]{:S(2)}, u32[]{:S(2)}) async-start(bf16[4,16,4,2,128]{4,2,3,0,1:T(4,128)(2,1)} %copy.399), calls=%async_computation.3 | async-start | bytes 262144 | tf_op jit(solution)/shard_map/all_to_all | solution.py:119
  243.1 4.0 slice_bitcast_fusion.1
  247.2 4.1 all-to-all-done.2
  251.4 3.4 reshape.84
  254.8 3.4 fusion.150
  274.8 3.3 fusion.27
  280.1 3.4 all-to-all-start.3
  284.7 6.7 %all-to-all-done.3 = bf16[4,2,32,2,128]{4,0,3,1,2:T(4,128)(2,1)S(1)} async-done(((bf16[4,2,32,2,128]{4,0,3,1,2:T(4,128)(2,1)}), bf16[4,2,32,2,128]{4,0,3,1,2:T(4,128)(2,1)S(1)}, u32[]{:S(2)}, u32[]{:S(2)}) %all-to-all-start.3) | async-done | bytes 131104 | tf_op jit(solution)/shard_map/all_to_all | solution.py:68
  291.5 3.6 reshape.86
  308.8 6.8 %fusion.81 = f32[256,8,1024]{2,0,1:T(8,128)S(1)} fusion(f32[4,2,8,1024]{3,0,2,1:T(4,128)S(1)} %fusion.69, s32[4]{0:T(128)S(1)} %iota_add_fusion, f32[4]{0:T(128)S(1)} %compare_select_fusion), kind=kOutput, calls=%fused_computation.100 | convolution fusion | flops 100678656 | bytes 8520704 | tf_op jit(solution)/shard_map/fvn,ft->nvt/dot_general | solution.py:88
  315.7 9.6 %subtract_bitcast_fusion = f32[1024,8,256]{0,2,1:T(8,128)} fusion(f32[256,8,1024]{2,0,1:T(8,128)S(1)} %fusion.81, f32[4,2,8,1024]{3,0,2,1:T(4,128)S(1)} %fusion.69, s32[4]{0:T(128)S(1)} %iota_add_fusion, f32[4]{0:T(128)S(1)} %compare_select_fusion), kind=kOutput, calls=%fused_computation | convolution fusion | flops 102775808 | bytes 16909312 | tf_op jit(solution)/shard_map/fvn,ft->nvt/dot_general | solution.py:89
  325.3 9.3 %copy.423 = f32[1024,8,256]{2,1,0:T(8,128)} copy(f32[1024,8,256]{0,2,1:T(8,128)} %subtract_bitcast_fusion) | data formatting | bytes 16777216 | tf_op jit(solution)/shard_map/sub | solution.py:88
  334.6 93.8 %reduce-scatter.5.cloned.1.call-done = f32[32,8,256]{2,1,0:T(8,128)} async-done(((f32[1024,8,256]{2,1,0:T(8,128)}), f32[32,8,256]{2,1,0:T(8,128)}) %reduce-scatter.5.cloned.1.call-update) | async-done | bytes 262160 | tf_op jit(solution)/shard_map/reduce_scatter | solution.py:87
  432.3 16.0 %all_to_all.81 = f32[32,1,2048]{2,1,0:T(1,128)S(1)} all-to-all(f32[32,1,2048]{2,1,0:T(1,128)S(1)} %reshape.111), channel_id=1, replica_groups=mesh['freq'=32,'tile'=8] {'freq'}, dimensions={0} | all-to-all | bytes 524288 | tf_op jit(solution)/shard_map/all_to_all | solution.py:102
  (147 shorter events, 82.0 us)
Async XLA Ops:
  8.3 1.1 copy-start.17
  9.5 8.5 %copy-start = (bf16[4,2,32,2,16,256]{5,4,3,2,1,0:T(8,128)(2,1)S(1)}, bf16[4,2,32,2,16,256]{5,4,3,2,1,0:T(8,128)(2,1)}, u32[]{:S(2)}) copy-start(bf16[4,2,32,2,16,256]{5,4,3,2,1,0:T(8,128)(2,1)} %param.7) | copy-start | bytes 12582916
  28.9 16.8 %all-to-all-start = ((bf16[4,2,32,2,128]{4,0,3,1,2:T(4,128)(2,1)}), bf16[4,2,32,2,128]{4,0,3,1,2:T(4,128)(2,1)S(1)}, u32[]{:S(2)}, u32[]{:S(2)}) async-start(bf16[4,2,32,2,128]{4,0,3,1,2:T(4,128)(2,1)} %copy.380), calls=%async_computation | async-start | bytes 262144 | tf_op jit(solution)/shard_map/all_to_all | solution.py:68
  37.9 147.7 %reduce-scatter.3.cloned.1.call-start = ((), (), s32[]{:S(2)}) async-start(), calls=%async_computation.7 | async-start | bytes 8650752 | tf_op jit(solution)/shard_map/reduce_scatter | solution.py:87
  42.2 171.9 %copy-start.1 = (bf16[4,16,4,1,16,256]{5,4,3,2,1,0:T(8,128)(2,1)}, bf16[4,16,4,1,16,256]{5,4,3,2,1,0:T(8,128)(2,1)S(1)}, u32[]{:S(2)}) copy-start(bf16[4,16,4,1,16,256]{5,4,3,2,1,0:T(8,128)(2,1)S(1)} %get-tuple-element.7) | copy-start | bytes 6291460
  57.2 2.6 copy-start.3
  57.2 2.6 copy-start.15
  60.5 1.1 copy-start.14
  61.2 1.1 copy-start.20
  88.2 97.4 %copy-start.19 = (f32[8]{0:T(128)S(1)}, f32[8]{0:T(128)}, u32[]{:S(2)}) copy-start(f32[8]{0:T(128)} %param.13) | copy-start | bytes 100
  88.2 99.3 %copy-start.21 = (f32[128]{0:T(128)}, f32[128]{0:T(128)S(1)}, u32[]{:S(2)}) copy-start(f32[128]{0:T(128)S(1)} %compare_select_fusion.1) | copy-start | bytes 1540
  190.1 16.7 %all-to-all-start.1 = ((f32[32,1,2048]{2,1,0:T(1,128)}), f32[32,1,2048]{2,1,0:T(1,128)S(1)}, u32[]{:S(2)}, u32[]{:S(2)}) async-start(f32[32,1,2048]{2,1,0:T(1,128)} %reshape.109), calls=%async_computation.2 | async-start | bytes 524288 | tf_op jit(solution)/shard_map/all_to_all | solution.py:102
  214.1 3.5 copy-start.4
  221.2 2.7 copy-start.5
  228.7 2.7 copy-start.10
  228.7 2.7 copy-start.11
  236.2 15.1 %all-to-all-start.2 = ((bf16[4,16,4,2,128]{4,2,3,0,1:T(4,128)(2,1)}), bf16[4,16,4,2,128]{4,2,3,0,1:T(4,128)(2,1)S(1)}, u32[]{:S(2)}, u32[]{:S(2)}) async-start(bf16[4,16,4,2,128]{4,2,3,0,1:T(4,128)(2,1)} %copy.399), calls=%async_computation.3 | async-start | bytes 262144 | tf_op jit(solution)/shard_map/all_to_all | solution.py:119
  262.8 2.5 copy-start.7
  262.8 2.5 copy-start.12
  266.0 1.5 copy-start.18
  267.5 3.8 copy-start.8
  271.3 3.5 copy-start.9
  280.1 11.2 %all-to-all-start.3 = ((bf16[4,2,32,2,128]{4,0,3,1,2:T(4,128)(2,1)}), bf16[4,2,32,2,128]{4,0,3,1,2:T(4,128)(2,1)S(1)}, u32[]{:S(2)}, u32[]{:S(2)}) async-start(bf16[4,2,32,2,128]{4,0,3,1,2:T(4,128)(2,1)} %copy.416), calls=%async_computation.4 | async-start | bytes 262144 | tf_op jit(solution)/shard_map/all_to_all | solution.py:68
  283.5 144.9 %reduce-scatter.5.cloned.1.call-start = ((), (), s32[]{:S(2)}) async-start(), calls=%async_computation.8 | async-start | bytes 8650752 | tf_op jit(solution)/shard_map/reduce_scatter | solution.py:87
  295.1 5.7 %copy-start.6 = (bf16[4,16,4,1,16,256]{5,4,3,2,1,0:T(8,128)(2,1)S(1)}, bf16[4,16,4,1,16,256]{5,4,3,2,1,0:T(8,128)(2,1)}, u32[]{:S(2)}) copy-start(bf16[4,16,4,1,16,256]{5,4,3,2,1,0:T(8,128)(2,1)} %get-tuple-element.8) | copy-start | bytes 6291460
  303.1 3.6 copy-start.2
  304.3 2.5 copy-start.16
  304.3 2.5 copy-start.23
  306.8 1.0 copy-start.13
  334.6 94.9 %copy-start.22 = (f32[128]{0:T(128)S(1)}, f32[128]{0:T(128)}, u32[]{:S(2)}) copy-start(f32[128]{0:T(128)} %copy-done.21) | copy-start | bytes 1540
Sparse Core Ops, SparseCore 0:
  88.3 97.1 reduce-scatter.2
  334.7 93.6 reduce-scatter.4
where the time goes:
time: 466 us; the launch traced here: 459 us
  waiting for transfers between devices  211 us (45%)
  matrix products  91.9 us (20%)
  local copies, waits for them, and re-layouts  89.2 us (19%)
  starting transfers between devices  27.5 us (6%)
  blocking collectives  16 us (3%)
  between operations  14.3 us (3%)
  other arithmetic  8.46 us (2%)
    reduce_scatter x2, waiting for transfers between devices, to_time(): lax.psum_scatter(jnp.einsum('fvn,ft->nvt', wavefield[:, 0], cos_own, prec...  190 us
    dot_general x8, matrix products, contract_left(): jnp.einsum('fijkq,fviq->fijkv', matrix, vectors, preferred_element_type=j...  25.6 us
    dot_general x2, matrix products, to_time(): jnp.einsum('fvn,ft->nvt', wavefield[:, 1], sin_own, precision=highest)  19.2 us
    sub x2, local copies, waits for them, and re-layouts, to_time(): jnp.einsum('fvn,ft->nvt', wavefield[:, 0], cos_own, precision=highest)  18.5 us
    unnamed x59, local copies, waits for them, and re-layouts  16.5 us
    all_to_all x1, blocking collectives, to_freq(): lax.all_to_all(jnp.stack([real_part, imag_part], 1), 'freq', split_axis=0...  16 us
    dot_general x4, matrix products, project(): jnp.einsum('fijkp,fvjp->fijkv', matrix, vectors, preferred_element_type=j...  14.4 us
    dot_general x2, matrix products, to_time(): jnp.einsum('fvn,ft->nvt', wavefield[:, 0], cos_own, precision=highest)  13.7 us
  transfers between devices with their start and end apart: 6, of which 6 were waited for; matrix products, arithmetic and copies ran while one was open for 2% of the time, Pallas kernels for 0%

commit v1 on v0

v1 whole, which is shorter than its diff:
```python
import functools
import math

import jax
import jax.numpy as jnp
import numpy as np
from jax import lax
from jax.experimental import pallas as pl
from jax.experimental.pallas import tpu as pltpu
from jax.sharding import PartitionSpec as P

F32 = jnp.float32
BF16 = jnp.bfloat16
HIGHEST = lax.Precision.HIGHEST
NT = (((1,), (1,)), ((), ()))
INTERPRET = False


class Sizes:
    def __init__(self, left, right, recorded, tiles, groups):
        self.freqs, self.rows, self.col_tiles, _, self.slots, self.side = left.shape
        self.row_tiles, self.cols = right.shape[1], right.shape[2]
        self.virtual = recorded.shape[2]
        self.tiles, self.groups = tiles, groups
        self.lanes = self.rows * self.cols * self.slots
        self.pairs = 2 * self.freqs
        self.times = 2 * self.freqs * groups
        assert self.lanes == 128 and self.virtual == 8 and self.tiles % 2 == 0
        assert self.groups == self.virtual * self.cols and self.slots == 16


def lane_group(z, shape, which):
    lane = lax.broadcasted_iota(jnp.int32, shape, 1) % z.lanes
    if which == 0:
        return lane // (z.cols * z.slots)
    return (lane // z.slots) % z.cols


def left_block(z, u, f, c, s):
    return u[f, :, z.cols * s : z.cols * (s + 1), c].reshape(z.lanes, z.side)


def right_block(z, v, f, c, s):
    return v[f, z.rows * s : z.rows * (s + 1), :, c].reshape(z.lanes, z.side)


def block_pair(block, z, ref, f, c, pair):
    return jnp.concatenate([block(z, ref, f, c, 2 * pair), block(z, ref, f, c, 2 * pair + 1)], 0)


def finish_weights(z, scales, ranks, expand):
    wide = jnp.dot(scales, expand, precision=HIGHEST, preferred_element_type=F32)
    live = jnp.dot(ranks, expand, precision=HIGHEST, preferred_element_type=F32)
    slot = (lax.broadcasted_iota(jnp.int32, wide.shape, 1) % z.slots).astype(F32)
    return jnp.where(slot < live, wide, 0.0)


def row_weights(z, here, ranks_ref, scales_ref, f):
    rows = []
    for source in (None, ranks_ref):
        parts = []
        for r in range(z.rows):
            at = pl.ds(z.rows * here + r, 1)
            if source is None:
                one = scales_ref[f, 0, at, :] * scales_ref[f, 1, at, :]
            else:
                one = ranks_ref[f, at, :].astype(F32)
            wide = jnp.broadcast_to(one, (z.tiles, z.col_tiles))
            owner = lax.broadcasted_iota(jnp.int32, wide.shape, 1) // z.cols
            mine = owner == lax.broadcasted_iota(jnp.int32, wide.shape, 0)
            parts.append(jnp.where(mine, wide, 0.0))
        rows.append(jnp.concatenate(parts, 1))
    shape = (z.rows * z.col_tiles, z.lanes)
    source_at = lax.broadcasted_iota(jnp.int32, shape, 0)
    same_row = source_at // z.col_tiles == lane_group(z, shape, 0)
    same_col = source_at % z.cols == lane_group(z, shape, 1)
    expand = jnp.where(same_row & same_col, 1.0, 0.0).astype(F32)
    return finish_weights(z, rows[0], rows[1], expand)


def column_weights(z, here, ranks_ref, scales_ref, f):
    rows = []
    for source in (None, ranks_ref):
        parts = []
        for r in range(z.rows):
            at = pl.ds(r, z.tiles, stride=z.rows)
            if source is None:
                parts.append(scales_ref[f, 0, at, :] * scales_ref[f, 1, at, :])
            else:
                parts.append(ranks_ref[f, at, :].astype(F32))
        rows.append(jnp.concatenate(parts, 1))
    shape = (z.rows * z.col_tiles, z.lanes)
    source_at = lax.broadcasted_iota(jnp.int32, shape, 0)
    same_row = source_at // z.col_tiles == lane_group(z, shape, 0)
    same_col = source_at % z.col_tiles == z.cols * here + lane_group(z, shape, 1)
    expand = jnp.where(same_row & same_col, 1.0, 0.0).astype(F32)
    return finish_weights(z, rows[0], rows[1], expand)


def contract(z, block, ref, f, vectors, which, weights, out_ref):
    first = jnp.concatenate([x for re, im in vectors for x in (re, im)], 0).astype(BF16)
    second = jnp.concatenate([x for re, im in vectors for x in (im, -re)], 0).astype(BF16)
    high = 2 * z.virtual
    group = lane_group(z, (high, 2 * z.lanes), which)
    for pair in range(z.tiles // 2):
        total = lax.dot_general(
            first, block_pair(block, z, ref, f, 0, pair), NT, preferred_element_type=F32
        ) + lax.dot_general(
            second, block_pair(block, z, ref, f, 1, pair), NT, preferred_element_type=F32
        )
        picked = total[:high]
        for at in range(1, len(vectors)):
            picked = jnp.where(group == at, total[at * high : (at + 1) * high], picked)
        for half in range(2):
            s = 2 * pair + half
            part = picked[:, half * z.lanes : (half + 1) * z.lanes] * weights[s : s + 1]
            out_ref[s, f] = part.astype(BF16)


def combine(z, block, ref, f, arrived_ref, which, count):
    total = None
    v = z.virtual
    for pair in range(z.tiles // 2):
        coefs = jnp.concatenate([arrived_ref[2 * pair, f], arrived_ref[2 * pair + 1, f]], 1).astype(F32)
        turned = jnp.concatenate([-coefs[v:], coefs[:v]], 0)
        group = lane_group(z, coefs.shape, which)
        for c, rows in enumerate((coefs, turned)):
            masked = jnp.concatenate([jnp.where(group == at, rows, 0.0) for at in range(count)], 0)
            part = jnp.dot(
                masked.astype(BF16), block_pair(block, z, ref, f, c, pair), preferred_element_type=F32
            )
            total = part if total is None else total + part
    return total


def fetch(z, hbm, vmem, sems):
    copies = [pltpu.make_async_copy(hbm.at[f], vmem.at[f], sems.at[f]) for f in range(z.freqs)]
    for copy in copies:
        copy.start()
    return copies


def first_duals_kernel(z, left_hbm, recorded_ref, ranks_ref, scales_ref, out_ref, u, sems):
    copies = fetch(z, left_hbm, u, sems)
    here = lax.axis_index("tile")
    for f in range(z.freqs):
        weights = row_weights(z, here, ranks_ref, scales_ref, f)
        vectors = []
        for r in range(z.rows):
            at = slice(r * z.side, (r + 1) * z.side)
            vectors.append((recorded_ref[f, 0, :, at], recorded_ref[f, 1, :, at]))
        copies[f].wait()
        contract(z, left_block, u, f, vectors, 0, weights, out_ref)


def source_rows(z, f, c, j, half):
    halves = z.side // 128
    start = (j * halves + half) * z.pairs + 2 * f + c
    return pl.ds(start, z.virtual, stride=z.cols * halves * z.pairs)


def gradient_kernel(z, with_first, right_hbm, arrived_ref, steps_ref, *refs):
    if with_first:
        first_ref, out_ref, v, sems = refs
    else:
        out_ref, v, sems = refs
    copies = fetch(z, right_hbm, v, sems)
    high = 2 * z.virtual
    for f in range(z.freqs):
        copies[f].wait()
        total = combine(z, right_block, v, f, arrived_ref, 1, z.cols) * steps_ref[f]
        for j in range(z.cols):
            for c in range(2):
                start = j * high + c * z.virtual
                rows = total[start : start + z.virtual]
                for half in range(z.side // 128):
                    at = source_rows(z, f, c, j, half)
                    part = rows[:, half * 128 : (half + 1) * 128]
                    out_ref[at, :] = first_ref[at, :] + part if with_first else part


def threshold_kernel(z, arrived_ref, table_ref, thresholds_ref, out_ref):
    table = table_ref[...]
    halves = z.side // 128
    fields = [arrived_ref[:, half].reshape(z.times, 128) for half in range(halves)]
    signal = jnp.dot(table, jnp.concatenate(fields, 1), precision=HIGHEST, preferred_element_type=F32)
    level = thresholds_ref[lax.axis_index("freq") // z.cols]
    kept = signal - jnp.clip(signal, -level, level)
    back = lax.dot_general(
        table, kept, (((0,), (0,)), ((), ())), precision=HIGHEST, preferred_element_type=F32
    )
    for half in range(halves):
        out_ref[:, half] = back[:, half * 128 : (half + 1) * 128].reshape(z.groups, z.pairs, 128)


def field_rows(z, ref, f, c, j):
    return jnp.concatenate([ref[source_rows(z, f, c, j, half), :] for half in range(z.side // 128)], 1)


def coefficients_kernel(z, right_hbm, field_ref, ranks_ref, scales_ref, out_ref, v, sems):
    copies = fetch(z, right_hbm, v, sems)
    here = lax.axis_index("tile")
    for f in range(z.freqs):
        weights = column_weights(z, here, ranks_ref, scales_ref, f)
        vectors = [(field_rows(z, field_ref, f, 0, j), field_rows(z, field_ref, f, 1, j)) for j in range(z.cols)]
        copies[f].wait()
        contract(z, right_block, v, f, vectors, 1, weights, out_ref)


def residual_kernel(z, left_hbm, arrived_ref, recorded_ref, ranks_ref, scales_ref, out_ref, u, sems):
    copies = fetch(z, left_hbm, u, sems)
    here = lax.axis_index("tile")
    v = z.virtual
    for f in range(z.freqs):
        weights = row_weights(z, here, ranks_ref, scales_ref, f)
        copies[f].wait()
        image = combine(z, left_block, u, f, arrived_ref, 0, z.rows)
        vectors = []
        for r in range(z.rows):
            at = slice(r * z.side, (r + 1) * z.side)
            start = 2 * r * v
            vectors.append(
                (
                    recorded_ref[f, 0, :, at] - image[start : start + v],
                    recorded_ref[f, 1, :, at] - image[start + v : start + 2 * v],
                )
            )
        contract(z, left_block, u, f, vectors, 0, weights, out_ref)


def output_kernel(z, field_ref, out_ref):
    for f in range(z.freqs):
        for c in range(2):
            for j in range(z.cols):
                out_ref[f, c, :, j * z.side : (j + 1) * z.side] = field_rows(z, field_ref, f, c, j)


def dft_table(freqs, times):
    f = np.arange(freqs)[:, None]
    t = np.arange(times)[None, :]
    angles = ((f * t) % times) * (2.0 * math.pi / times)
    scaling = np.where(f == 0, math.sqrt(1.0 / times), math.sqrt(2.0 / times))
    both = np.stack([scaling * np.cos(angles), -scaling * np.sin(angles)], 1)
    return np.ascontiguousarray(both.reshape(2 * freqs, times).T.astype(np.float32))


HBM = pl.BlockSpec(memory_space=pl.ANY)
VMEM = pl.BlockSpec(memory_space=pltpu.VMEM)
SMEM = pl.BlockSpec(memory_space=pltpu.SMEM)


def run(name, kernel, in_specs, out, scratch=()):
    return pl.pallas_call(
        kernel,
        name=name,
        in_specs=in_specs,
        out_specs=VMEM,
        out_shape=out,
        scratch_shapes=list(scratch),
        interpret=INTERPRET,
        compiler_params=pltpu.CompilerParams(vmem_limit_bytes=40 << 20),
    )


def per_device(left, right, tile_ranks, tile_scales, recorded, step_sizes, thresholds, tiles, groups):
    z = Sizes(left, right, recorded, tiles, groups)
    held_left = [pltpu.VMEM(left.shape, BF16), pltpu.SemaphoreType.DMA((z.freqs,))]
    held_right = [pltpu.VMEM(right.shape, BF16), pltpu.SemaphoreType.DMA((z.freqs,))]
    coefs = jax.ShapeDtypeStruct((z.tiles, z.freqs, 2 * z.virtual, z.lanes), BF16)
    halves = z.side // 128
    rows = z.groups * halves * z.pairs
    field = jax.ShapeDtypeStruct((rows, 128), F32)
    blocks = jax.ShapeDtypeStruct((z.groups, halves, z.pairs, 128), F32)
    table = jnp.asarray(dft_table(z.freqs * z.groups, z.times))

    def over_tile(x):
        return lax.all_to_all(x, "tile", split_axis=0, concat_axis=0, tiled=True)

    def over_freq(x):
        return lax.all_to_all(x.reshape(blocks.shape), "freq", split_axis=0, concat_axis=0, tiled=True)

    part = functools.partial
    duals = run("first_duals", part(first_duals_kernel, z), [HBM, VMEM, VMEM, VMEM], coefs, held_left)(
        left, recorded, tile_ranks, tile_scales
    )
    update = run("first_gradient", part(gradient_kernel, z, False), [HBM, VMEM, SMEM], field, held_right)(
        right, over_tile(duals), step_sizes
    )
    shrink = run("threshold", part(threshold_kernel, z), [VMEM, VMEM, SMEM], blocks)
    first = over_freq(shrink(over_freq(update), table, thresholds)).reshape(rows, 128)
    coeffs = run("coefficients", part(coefficients_kernel, z), [HBM, VMEM, VMEM, VMEM], coefs, held_right)(
        right, first, tile_ranks, tile_scales
    )
    duals = run("residual", part(residual_kernel, z), [HBM, VMEM, VMEM, VMEM, VMEM], coefs, held_left)(
        left, over_tile(coeffs), recorded, tile_ranks, tile_scales
    )
    update = run("second_gradient", part(gradient_kernel, z, True), [HBM, VMEM, SMEM, VMEM], field, held_right)(
        right, over_tile(duals), step_sizes, first
    )
    second = over_freq(shrink(over_freq(update), table, thresholds)).reshape(rows, 128)
    out = jax.ShapeDtypeStruct((z.freqs, 2, z.virtual, z.cols * z.side), F32)
    return run("output", part(output_kernel, z), [VMEM], out)(second)


def solution(mesh):
    return jax.shard_map(
        functools.partial(per_device, tiles=mesh.shape["tile"], groups=mesh.shape["freq"]),
        mesh=mesh,
        in_specs=(
            P("freq", "tile", None, None, None, None),
            P("freq", None, "tile", None, None, None),
            P("freq", None, None),
            P("freq", None, None, None),
            P("freq", None, None, "tile"),
            P("freq"),
            P(),
        ),
        out_specs=P("freq", None, None, "tile"),
        check_vma=False,
    )
```

time: 466 us -> 121 us (0.26); the launches traced: 459 us -> 120 us
  waiting for transfers between devices: 211 us -> 0 us
  matrix products: 91.9 us -> 0 us
  local copies, waits for them, and re-layouts: 89.2 us -> 5.06 us
  blocking collectives: 16 us -> 96.4 us
  starting transfers between devices: 27.5 us -> 0 us
  Pallas kernels: 0 us -> 18.6 us
  between operations: 14.3 us -> 0.1 us
  other arithmetic: 8.46 us -> 0 us
    reduce_scatter x2 -> x0, waiting for transfers between devices: 190 us -> none  [to_time(): lax.psum_scatter(jnp.einsum('fvn,ft->nvt', wavefield[:, 0], cos_own, prec...]
    dot_general x32 -> x0, matrix products: 91.9 us -> none  [the longest x8 25.6 us: contract_left(): jnp.einsum('fijkq,fviq->fijkv', matrix, vectors, preferred_element_type=j...]
    all_to_all x1 -> x7, blocking collectives: 16 us -> 96.4 us  [the longest x4 58.3 us: over_freq(): lax.all_to_all(x.reshape(blocks.shape), 'freq', split_axis=0, concat_axis...]
    all_to_all x4 -> x0, starting transfers between devices: 27.2 us -> none  [the longest x2 12.4 us: gradient(): lax.all_to_all(duals, 'tile', split_axis=2, concat_axis=1, tiled=True)]
    sub x5 -> x0, local copies, waits for them, and re-layouts: 21.7 us -> none  [the longest x2 18.5 us: to_time(): jnp.einsum('fvn,ft->nvt', wavefield[:, 0], cos_own, precision=highest)]
    all_to_all x4 -> x0, waiting for transfers between devices: 21 us -> none  [the longest x2 10.1 us: gradient(): lax.all_to_all(duals, 'tile', split_axis=2, concat_axis=1, tiled=True)]
    pallas_call x0 -> x8, Pallas kernels: none -> 18.6 us  [the longest x1 4.14 us: per_device(): run('residual', part(residual_kernel, z), [HBM, VMEM, VMEM, VMEM, VMEM],...]
    slice x7 -> x0, local copies, waits for them, and re-layouts: 14.2 us -> none  [the longest x2 6.63 us: gradient(): arrived[:, :, :, 1]]
  transfers between devices with their start and end apart: 6 -> 0, of which waited for: 6 -> 0; matrix products, arithmetic and copies ran while one was open for 2% -> 0% of each run, Pallas kernels for 0% -> 0%
where the time goes in v1:
time: 121 us; the launch traced here: 120 us
  blocking collectives  96.4 us (80%)
  Pallas kernels  18.6 us (15%)
  local copies, waits for them, and re-layouts  5.06 us (4%)
    all_to_all x4, blocking collectives, over_freq(): lax.all_to_all(x.reshape(blocks.shape), 'freq', split_axis=0, concat_axis...  58.3 us
    all_to_all x3, blocking collectives, over_tile(): return lax.all_to_all(x, 'tile', split_axis=0, concat_axis=0, tiled=True)  38 us
    unnamed x24, local copies, waits for them, and re-layouts  5.06 us
    pallas_call x1, Pallas kernels, per_device(): run('residual', part(residual_kernel, z), [HBM, VMEM, VMEM, VMEM, VMEM],...  4.14 us
    pallas_call x2, Pallas kernels, per_device(): shrink(over_freq(update), table, thresholds)  3.25 us
    pallas_call x1, Pallas kernels, per_device(): run('second_gradient', part(gradient_kernel, z, True), [HBM, VMEM, SMEM,...  2.68 us
    pallas_call x1, Pallas kernels, per_device(): run('first_gradient', part(gradient_kernel, z, False), [HBM, VMEM, SMEM],...  2.68 us
    pallas_call x1, Pallas kernels, per_device(): run('coefficients', part(coefficients_kernel, z), [HBM, VMEM, VMEM, VMEM]...  2.56 us

profile of v1, /device:TPU:1, one launch (start us, length us, event | category | flops | bytes accessed | tf_op | source)
XLA Modules:
  0.0 120.1 jit_solution(4710438160888658463)
XLA Ops:
  0.0 0.0 copy-start
  0.0 2.3 %copy-done.1 = bf16[4,2,32,2,16,256]{5,4,3,2,1,0:T(8,128)(2,1)S(1)} copy-done((bf16[4,2,32,2,16,256]{5,4,3,2,1,0:T(8,128)(2,1)S(1)}, bf16[4,2,32,2,16,256]{5,4,3,2,1,0:T(8,128)(2,1)}, u32[]{:S(2)}) %copy-start.1) | copy-done | bytes 4194328
  2.3 1.0 copy-done.4
  3.4 0.9 copy-done.6
  4.3 0.8 copy-done.8
  5.0 2.4 %first_duals.1 = bf16[8,4,16,128]{3,2,1,0:T(8,128)(2,1)S(1)} custom-call(bf16[4,2,32,2,16,256]{5,4,3,2,1,0:T(8,128)(2,1)S(1)} %copy-done.1, f32[4,2,8,512]{3,2,1,0:T(8,128)S(1)} %copy-done.6, s32[4,16,32]{2,1,0:T(8,128)S(1)} %copy-done.8, f32[4,2,16,32]{3,2,1,0:T(8,128)S(1)} %copy-done.4), custom_call_target="tpu_custom_call" | custom-call | tf_op jit(solution)/shard_map/first_duals/pallas_call | solution.py:283
  7.4 0.0 copy-start.5
  7.5 0.0 copy-start.9
  7.5 16.7 %all_to_all.35.arrived_ref = bf16[8,4,16,128]{3,2,1,0:T(8,128)(2,1)S(1)} all-to-all(bf16[8,4,16,128]{3,2,1,0:T(8,128)(2,1)S(1)} %first_duals.1), channel_id=1, replica_groups=mesh['freq'=32,'tile'=8] {'tile'}, dimensions={0} | all-to-all | bytes 262144 | tf_op jit(solution)/shard_map/all_to_all | solution.py:277
  24.2 0.0 copy-done
  24.2 0.0 copy-done.10
  24.2 2.7 %first_gradient.1 = f32[512,128]{1,0:T(8,128)S(1)} custom-call(bf16[4,16,4,2,16,256]{5,4,3,2,1,0:T(8,128)(2,1)S(1)} %copy-done, bf16[8,4,16,128]{3,2,1,0:T(8,128)(2,1)S(1)} %all_to_all.35.arrived_ref, f32[4]{0:T(128)S(1)} %copy-done.10), custom_call_target="tpu_custom_call" | custom-call | tf_op jit(solution)/shard_map/first_gradient/pallas_call | solution.py:286
  26.9 0.0 copy-start.2
  26.9 0.0 copy-start.7
  26.9 18.3 %all_to_all.36.arrived_ref = f32[32,2,8,128]{3,2,1,0:T(8,128)S(1)} all-to-all(f32[32,2,8,128]{3,2,1,0:T(8,128)S(1)} %bitcast.7), channel_id=1, replica_groups=mesh['freq'=32,'tile'=8] {'freq'}, dimensions={0} | all-to-all | bytes 524288 | tf_op jit(solution)/shard_map/all_to_all | solution.py:280
  45.2 0.0 copy-done.3
  45.2 0.0 copy-done.11
  45.2 1.6 %threshold.2 = f32[32,2,8,128]{3,2,1,0:T(8,128)S(1)} custom-call(f32[32,2,8,128]{3,2,1,0:T(8,128)S(1)} %all_to_all.36.arrived_ref, f32[256,256]{1,0:T(8,128)S(1)} %copy-done.3, f32[8]{0:T(128)S(1)} %copy-done.11), custom_call_target="tpu_custom_call" | custom-call | tf_op jit(solution)/shard_map/threshold/pallas_call | solution.py:290
  46.9 12.5 %all_to_all.37 = f32[32,2,8,128]{3,2,1,0:T(8,128)S(1)} all-to-all(f32[32,2,8,128]{3,2,1,0:T(8,128)S(1)} %threshold.2), channel_id=1, replica_groups=mesh['freq'=32,'tile'=8] {'freq'}, dimensions={0} | all-to-all | bytes 524288 | tf_op jit(solution)/shard_map/all_to_all | solution.py:280
  59.3 0.0 copy-done.5
  59.3 0.0 copy-done.9
  59.3 2.6 %coefficients.1 = bf16[8,4,16,128]{3,2,1,0:T(8,128)(2,1)S(1)} custom-call(bf16[4,16,4,2,16,256]{5,4,3,2,1,0:T(8,128)(2,1)S(1)} %copy-done, f32[512,128]{1,0:T(8,128)S(1)} %bitcast.4, s32[4,16,32]{2,1,0:T(8,128)S(1)} %copy-done.9, f32[4,2,16,32]{3,2,1,0:T(8,128)S(1)} %copy-done.5), custom_call_target="tpu_custom_call" | custom-call | tf_op jit(solution)/shard_map/coefficients/pallas_call | solution.py:291
  61.9 10.9 %all_to_all.38.arrived_ref = bf16[8,4,16,128]{3,2,1,0:T(8,128)(2,1)S(1)} all-to-all(bf16[8,4,16,128]{3,2,1,0:T(8,128)(2,1)S(1)} %coefficients.1), channel_id=1, replica_groups=mesh['freq'=32,'tile'=8] {'tile'}, dimensions={0} | all-to-all | bytes 262144 | tf_op jit(solution)/shard_map/all_to_all | solution.py:277
  72.8 0.0 copy-done.2
  72.8 0.0 copy-done.7
  72.8 4.1 %residual.1 = bf16[8,4,16,128]{3,2,1,0:T(8,128)(2,1)S(1)} custom-call(bf16[4,2,32,2,16,256]{5,4,3,2,1,0:T(8,128)(2,1)S(1)} %copy-done.2, bf16[8,4,16,128]{3,2,1,0:T(8,128)(2,1)S(1)} %all_to_all.38.arrived_ref, f32[4,2,8,512]{3,2,1,0:T(8,128)S(1)} %copy-done.7, s32[4,16,32]{2,1,0:T(8,128)S(1)} %copy-done.9, f32[4,2,16,32]{3,2,1,0:T(8,128)S(1)} %copy-done.5), custom_call_target="tpu_custom_call" | custom-call | tf_op jit(solution)/shard_map/residual/pallas_call | solution.py:294
  77.0 10.4 %all_to_all.39.arrived_ref = bf16[8,4,16,128]{3,2,1,0:T(8,128)(2,1)S(1)} all-to-all(bf16[8,4,16,128]{3,2,1,0:T(8,128)(2,1)S(1)} %residual.1), channel_id=1, replica_groups=mesh['freq'=32,'tile'=8] {'tile'}, dimensions={0} | all-to-all | bytes 262144 | tf_op jit(solution)/shard_map/all_to_all | solution.py:277
  87.4 2.7 %second_gradient.1 = f32[512,128]{1,0:T(8,128)S(1)} custom-call(bf16[4,16,4,2,16,256]{5,4,3,2,1,0:T(8,128)(2,1)S(1)} %copy-done, bf16[8,4,16,128]{3,2,1,0:T(8,128)(2,1)S(1)} %all_to_all.39.arrived_ref, f32[4]{0:T(128)S(1)} %copy-done.10, f32[512,128]{1,0:T(8,128)S(1)} %bitcast.5), custom_call_target="tpu_custom_call" | custom-call | tf_op jit(solution)/shard_map/second_gradient/pallas_call | solution.py:297
  90.1 15.1 %all_to_all.40.arrived_ref = f32[32,2,8,128]{3,2,1,0:T(8,128)S(1)} all-to-all(f32[32,2,8,128]{3,2,1,0:T(8,128)S(1)} %bitcast.6), channel_id=1, replica_groups=mesh['freq'=32,'tile'=8] {'freq'}, dimensions={0} | all-to-all | bytes 524288 | tf_op jit(solution)/shard_map/all_to_all | solution.py:280
  105.2 1.6 %threshold.3 = f32[32,2,8,128]{3,2,1,0:T(8,128)S(1)} custom-call(f32[32,2,8,128]{3,2,1,0:T(8,128)S(1)} %all_to_all.40.arrived_ref, f32[256,256]{1,0:T(8,128)S(1)} %copy-done.3, f32[8]{0:T(128)S(1)} %copy-done.11), custom_call_target="tpu_custom_call" | custom-call | tf_op jit(solution)/shard_map/threshold/pallas_call | solution.py:300
  106.8 12.5 %all_to_all.41 = f32[32,2,8,128]{3,2,1,0:T(8,128)S(1)} all-to-all(f32[32,2,8,128]{3,2,1,0:T(8,128)S(1)} %threshold.3), channel_id=1, replica_groups=mesh['freq'=32,'tile'=8] {'freq'}, dimensions={0} | all-to-all | bytes 524288 | tf_op jit(solution)/shard_map/all_to_all | solution.py:280
  119.2 0.9 output.1
  (7 shorter events, 0.0 us)
Async XLA Ops:
  0.0 24.2 %copy-start = (bf16[4,16,4,2,16,256]{5,4,3,2,1,0:T(8,128)(2,1)S(1)}, bf16[4,16,4,2,16,256]{5,4,3,2,1,0:T(8,128)(2,1)}, u32[]{:S(2)}) copy-start(bf16[4,16,4,2,16,256]{5,4,3,2,1,0:T(8,128)(2,1)} %right_hbm.5) | copy-start | bytes 12582916
  0.0 2.3 %copy-start.1 = (bf16[4,2,32,2,16,256]{5,4,3,2,1,0:T(8,128)(2,1)S(1)}, bf16[4,2,32,2,16,256]{5,4,3,2,1,0:T(8,128)(2,1)}, u32[]{:S(2)}) copy-start(bf16[4,2,32,2,16,256]{5,4,3,2,1,0:T(8,128)(2,1)} %left_hbm.3) | copy-start | bytes 12582916
  2.3 1.0 copy-start.4
  3.4 0.9 copy-start.6
  4.3 0.8 copy-start.8
  5.0 19.2 %copy-start.10 = (f32[4]{0:T(128)S(1)}, f32[4]{0:T(128)}, u32[]{:S(2)}) copy-start(f32[4]{0:T(128)} %steps_ref.3) | copy-start | bytes 52
  5.0 40.2 %copy-start.3 = (f32[256,256]{1,0:T(8,128)S(1)}, f32[256,256]{1,0:T(8,128)}, u32[]{:S(2)}) copy-start(f32[256,256]{1,0:T(8,128)} %constant.2.clone.table_ref) | copy-start | bytes 786436
  5.0 40.2 %copy-start.11 = (f32[8]{0:T(128)S(1)}, f32[8]{0:T(128)}, u32[]{:S(2)}) copy-start(f32[8]{0:T(128)} %thresholds_ref.3) | copy-start | bytes 100
  7.4 51.9 %copy-start.5 = (f32[4,2,16,32]{3,2,1,0:T(8,128)S(1)}, f32[4,2,16,32]{3,2,1,0:T(8,128)}, u32[]{:S(2)}) copy-start(f32[4,2,16,32]{3,2,1,0:T(8,128)} %scales_ref.5) | copy-start | bytes 49156
  7.5 51.9 %copy-start.9 = (s32[4,16,32]{2,1,0:T(8,128)S(1)}, s32[4,16,32]{2,1,0:T(8,128)}, u32[]{:S(2)}) copy-start(s32[4,16,32]{2,1,0:T(8,128)} %ranks_ref.5) | copy-start | bytes 24580
  26.9 46.0 %copy-start.2 = (bf16[4,2,32,2,16,256]{5,4,3,2,1,0:T(8,128)(2,1)S(1)}, bf16[4,2,32,2,16,256]{5,4,3,2,1,0:T(8,128)(2,1)}, u32[]{:S(2)}) copy-start(bf16[4,2,32,2,16,256]{5,4,3,2,1,0:T(8,128)(2,1)} %left_hbm.3) | copy-start | bytes 12582916
  26.9 45.9 %copy-start.7 = (f32[4,2,8,512]{3,2,1,0:T(8,128)S(1)}, f32[4,2,8,512]{3,2,1,0:T(8,128)}, u32[]{:S(2)}) copy-start(f32[4,2,8,512]{3,2,1,0:T(8,128)} %recorded_ref.3) | copy-start | bytes 393220

commit v2 on v1

v2 whole, which is shorter than its diff:
```python
import functools
import math

import jax
import jax.numpy as jnp
import ml_dtypes
import numpy as np
from jax import lax
from jax.experimental import pallas as pl
from jax.experimental.pallas import tpu as pltpu
from jax.sharding import PartitionSpec as P

F32 = jnp.float32
BF16 = jnp.bfloat16
HIGHEST = lax.Precision.HIGHEST
NT = (((1,), (1,)), ((), ()))
INTERPRET = False


class Sizes:
    def __init__(self, left, right, recorded, tiles, groups):
        self.freqs, self.rows, self.col_tiles, _, self.slots, self.side = left.shape
        self.row_tiles, self.cols = right.shape[1], right.shape[2]
        self.virtual = recorded.shape[2]
        self.tiles, self.groups = tiles, groups
        self.lanes = self.rows * self.cols * self.slots
        self.pairs = 2 * self.freqs
        self.times = 2 * self.freqs * groups
        assert self.lanes == 128 and self.virtual == 8 and self.tiles % 2 == 0
        assert self.groups == self.virtual * self.cols and self.slots == 16


def lane_group(z, shape, which):
    lane = lax.broadcasted_iota(jnp.int32, shape, 1) % z.lanes
    if which == 0:
        return lane // (z.cols * z.slots)
    return (lane // z.slots) % z.cols


def left_block(z, u, f, c, s):
    return u[f, :, z.cols * s : z.cols * (s + 1), c].reshape(z.lanes, z.side)


def right_block(z, v, f, c, s):
    return v[f, z.rows * s : z.rows * (s + 1), :, c].reshape(z.lanes, z.side)


def block_pair(block, z, ref, f, c, pair):
    return jnp.concatenate([block(z, ref, f, c, 2 * pair), block(z, ref, f, c, 2 * pair + 1)], 0)


def expand_weights(z, scales, ranks, expand):
    wide = jnp.dot(scales, expand, precision=HIGHEST, preferred_element_type=F32)
    live = jnp.dot(ranks.astype(BF16), expand.astype(BF16), preferred_element_type=F32)
    slot = (lax.broadcasted_iota(jnp.int32, wide.shape, 1) % z.slots).astype(F32)
    return jnp.where(slot < live, wide, 0.0)


def row_weights(z, here, ranks_ref, scales_ref):
    tables = []
    for scales in (True, False):
        rows = []
        for f in range(z.freqs):
            parts = []
            for r in range(z.rows):
                at = pl.ds(z.rows * here + r, 1)
                if scales:
                    one = scales_ref[f, 0, at, :] * scales_ref[f, 1, at, :]
                else:
                    one = ranks_ref[f, at, :].astype(F32)
                wide = jnp.broadcast_to(one, (z.tiles, z.col_tiles))
                owner = lax.broadcasted_iota(jnp.int32, wide.shape, 1) // z.cols
                mine = owner == lax.broadcasted_iota(jnp.int32, wide.shape, 0)
                parts.append(jnp.where(mine, wide, 0.0))
            rows.append(jnp.concatenate(parts, 1))
        tables.append(jnp.concatenate(rows, 0))
    shape = (z.rows * z.col_tiles, z.lanes)
    source_at = lax.broadcasted_iota(jnp.int32, shape, 0)
    same_row = source_at // z.col_tiles == lane_group(z, shape, 0)
    same_col = source_at % z.cols == lane_group(z, shape, 1)
    return expand_weights(z, *tables, jnp.where(same_row & same_col, 1.0, 0.0).astype(F32))


def column_weights(z, here, ranks_ref, scales_ref):
    tables = []
    for scales in (True, False):
        rows = []
        for f in range(z.freqs):
            parts = []
            for r in range(z.rows):
                at = pl.ds(r, z.tiles, stride=z.rows)
                if scales:
                    parts.append(scales_ref[f, 0, at, :] * scales_ref[f, 1, at, :])
                else:
                    parts.append(ranks_ref[f, at, :].astype(F32))
            rows.append(jnp.concatenate(parts, 1))
        tables.append(jnp.concatenate(rows, 0))
    shape = (z.rows * z.col_tiles, z.lanes)
    source_at = lax.broadcasted_iota(jnp.int32, shape, 0)
    same_row = source_at // z.col_tiles == lane_group(z, shape, 0)
    same_col = source_at % z.col_tiles == z.cols * here + lane_group(z, shape, 1)
    return expand_weights(z, *tables, jnp.where(same_row & same_col, 1.0, 0.0).astype(F32))


def contract(z, block, ref, f, vectors, which, weights_ref, out_ref):
    straight = jnp.concatenate([x for re, im in vectors for x in (re, im)], 0)
    turned = jnp.concatenate([x for re, im in vectors for x in (im, -re)], 0)
    both = jnp.concatenate([straight, turned], 1).astype(BF16)
    high = 2 * z.virtual
    group = lane_group(z, (high, 2 * z.lanes), which)
    for pair in range(z.tiles // 2):
        parts = [block_pair(block, z, ref, f, c, pair) for c in range(2)]
        total = lax.dot_general(both, jnp.concatenate(parts, 1), NT, preferred_element_type=F32)
        picked = total[:high]
        for at in range(1, len(vectors)):
            picked = jnp.where(group == at, total[at * high : (at + 1) * high], picked)
        for half in range(2):
            s = 2 * pair + half
            weight = weights_ref[f * z.tiles + s : f * z.tiles + s + 1, :]
            out_ref[s, f] = (picked[:, half * z.lanes : (half + 1) * z.lanes] * weight).astype(BF16)


def combine(z, block, ref, f, arrived_ref, which, count):
    total = None
    v = z.virtual
    for pair in range(z.tiles // 2):
        coefs = jnp.concatenate([arrived_ref[2 * pair, f], arrived_ref[2 * pair + 1, f]], 1).astype(F32)
        turned = jnp.concatenate([-coefs[v:], coefs[:v]], 0)
        group = lane_group(z, coefs.shape, which)
        sides = []
        for rows in (coefs, turned):
            sides.append(jnp.concatenate([jnp.where(group == at, rows, 0.0) for at in range(count)], 0))
        parts = [block_pair(block, z, ref, f, c, pair) for c in range(2)]
        part = jnp.dot(
            jnp.concatenate(sides, 1).astype(BF16), jnp.concatenate(parts, 0), preferred_element_type=F32
        )
        total = part if total is None else total + part
    return total


def first_duals_kernel(
    z, left_hbm, recorded_hbm, ranks_hbm, scales_hbm, steps_hbm, levels_hbm, out_ref, row_ref, col_ref, scalars_ref,
    u, recorded, ranks, scales, steps, levels, sems, small,
):
    here = lax.axis_index("tile")
    little = [
        pltpu.make_async_copy(source, target, small.at[n])
        for n, (source, target) in enumerate(
            (
                (ranks_hbm, ranks),
                (scales_hbm, scales),
                (recorded_hbm, recorded),
                (steps_hbm, steps),
                (levels_hbm, levels),
            )
        )
    ]
    wide = z.col_tiles // 4
    copies = [
        [
            pltpu.make_async_copy(
                left_hbm.at[f, r, pl.ds(q * wide, wide)], u.at[f, r, pl.ds(q * wide, wide)], sems.at[f, r, q]
            )
            for r in range(z.rows)
            for q in range(4)
        ]
        for f in range(z.freqs)
    ]
    for copy in little + [copy for group in copies for copy in group]:
        copy.start()
    little[0].wait()
    little[1].wait()
    row_ref[...] = row_weights(z, here, ranks, scales)
    col_ref[...] = column_weights(z, here, ranks, scales)
    for copy in little[2:]:
        copy.wait()
    at = lax.broadcasted_iota(jnp.int32, scalars_ref.shape, 0)
    scalars = jnp.full(scalars_ref.shape, levels[lax.axis_index("freq") // z.cols], F32)
    for f in range(z.freqs):
        scalars = jnp.where(at == f, steps[f], scalars)
    scalars_ref[...] = scalars
    for f in range(z.freqs):
        vectors = []
        for r in range(z.rows):
            at = slice(r * z.side, (r + 1) * z.side)
            vectors.append((recorded[f, 0, :, at], recorded[f, 1, :, at]))
        for copy in copies[f]:
            copy.wait()
        contract(z, left_block, u, f, vectors, 0, row_ref, out_ref)


def source_rows(z, f, c, j, half):
    halves = z.side // 128
    start = (j * halves + half) * z.pairs + 2 * f + c
    return pl.ds(start, z.virtual, stride=z.cols * halves * z.pairs)


def gradient(z, right, f, arrived_ref, scalars_ref, rows_ref):
    high = 2 * z.virtual
    total = combine(z, right_block, right, f, arrived_ref, 1, z.cols)
    for j in range(z.cols):
        for c in range(2):
            start = j * high + c * z.virtual
            for half in range(z.side // 128):
                part = total[start : start + z.virtual, half * 128 : (half + 1) * 128]
                rows_ref[source_rows(z, f, c, j, half), :] = part * scalars_ref[f : f + 1, :]


def first_gradient_kernel(z, right, arrived_ref, scalars_ref, out_ref):
    for f in range(z.freqs):
        gradient(z, right, f, arrived_ref, scalars_ref, out_ref)


def second_gradient_kernel(z, right, arrived_ref, scalars_ref, out_ref, rows_ref):
    for f in range(z.freqs):
        gradient(z, right, f, arrived_ref, scalars_ref, rows_ref)
    out_ref[...] = rows_ref[...].reshape(out_ref.shape).astype(BF16)


def times(tables_ref, which, x):
    high = x.astype(BF16)
    low = (x - high.astype(F32)).astype(BF16)
    return jnp.dot(tables_ref[which], jnp.concatenate([high, low, high], 0), preferred_element_type=F32)


def threshold(z, field, tables_ref, scalars_ref, out_ref):
    halves = z.side // 128
    signal = times(tables_ref, 0, field)
    level = jnp.concatenate([scalars_ref[z.freqs : z.freqs + 1, :]] * halves, 1)
    back = times(tables_ref, 1, signal - jnp.clip(signal, -level, level))
    parts = [back[:, half * 128 : (half + 1) * 128].reshape(z.groups, z.pairs, 128) for half in range(halves)]
    out_ref[...] = jnp.concatenate(parts, 1).astype(BF16)
    return back


def field_of(z, blocks):
    halves = z.side // 128
    parts = [blocks[:, half * z.pairs : (half + 1) * z.pairs].reshape(z.times, 128) for half in range(halves)]
    return jnp.concatenate(parts, 1)


def first_threshold_kernel(z, arrived_ref, tables_ref, scalars_ref, out_ref, first_ref):
    first_ref[...] = threshold(z, field_of(z, arrived_ref[...]), tables_ref, scalars_ref, out_ref)


def second_threshold_kernel(z, arrived_ref, first_ref, tables_ref, scalars_ref, out_ref):
    field = first_ref[...] + field_of(z, arrived_ref[...].astype(F32))
    threshold(z, field, tables_ref, scalars_ref, out_ref)


def field_rows(z, ref, f, c, j):
    return jnp.concatenate([ref[source_rows(z, f, c, j, half), :] for half in range(z.side // 128)], 1)


def coefficients_kernel(z, right, field_ref, weights_ref, out_ref, rows_ref):
    rows_ref[...] = field_ref[...].astype(F32).reshape(rows_ref.shape)
    for f in range(z.freqs):
        vectors = [(field_rows(z, rows_ref, f, 0, j), field_rows(z, rows_ref, f, 1, j)) for j in range(z.cols)]
        contract(z, right_block, right, f, vectors, 1, weights_ref, out_ref)


def residual_kernel(z, left, arrived_ref, recorded_ref, weights_ref, out_ref):
    v = z.virtual
    for f in range(z.freqs):
        image = combine(z, left_block, left, f, arrived_ref, 0, z.rows)
        vectors = []
        for r in range(z.rows):
            at = slice(r * z.side, (r + 1) * z.side)
            start = 2 * r * v
            vectors.append(
                (
                    recorded_ref[f, 0, :, at] - image[start : start + v],
                    recorded_ref[f, 1, :, at] - image[start + v : start + 2 * v],
                )
            )
        contract(z, left_block, left, f, vectors, 0, weights_ref, out_ref)


def output_kernel(z, field_ref, out_ref, rows_ref):
    rows_ref[...] = field_ref[...].astype(F32).reshape(rows_ref.shape)
    for f in range(z.freqs):
        for c in range(2):
            for j in range(z.cols):
                out_ref[f, c, :, j * z.side : (j + 1) * z.side] = field_rows(z, rows_ref, f, c, j)


def dft_tables(freqs, times):
    f = np.arange(freqs)[:, None]
    t = np.arange(times)[None, :]
    angles = ((f * t) % times) * (2.0 * math.pi / times)
    scaling = np.where(f == 0, math.sqrt(1.0 / times), math.sqrt(2.0 / times))
    both = np.stack([scaling * np.cos(angles), -scaling * np.sin(angles)], 1)
    forth = np.ascontiguousarray(both.reshape(2 * freqs, times).T.astype(np.float32))
    sides = []
    for table in (forth, forth.T):
        high = table.astype(ml_dtypes.bfloat16)
        low = (table - high.astype(np.float32)).astype(ml_dtypes.bfloat16)
        sides.append(np.concatenate([high, high, low], 1))
    return np.stack(sides)


HBM = pl.BlockSpec(memory_space=pltpu.HBM)
VMEM = pl.BlockSpec(memory_space=pltpu.VMEM)


def run(name, kernel, in_specs, out, scratch=()):
    return pl.pallas_call(
        kernel,
        name=name,
        in_specs=in_specs,
        out_specs=VMEM if isinstance(out, jax.ShapeDtypeStruct) else [VMEM] * len(out),
        out_shape=out,
        scratch_shapes=list(scratch),
        interpret=INTERPRET,
        compiler_params=pltpu.CompilerParams(vmem_limit_bytes=40 << 20),
    )


def per_device(left, right, tile_ranks, tile_scales, recorded, step_sizes, thresholds, tiles, groups):
    z = Sizes(left, right, recorded, tiles, groups)
    part = functools.partial
    shape = jax.ShapeDtypeStruct
    halves = z.side // 128
    coefs = shape((z.tiles, z.freqs, 2 * z.virtual, z.lanes), BF16)
    weights = shape((z.freqs * z.tiles, z.lanes), F32)
    rows = (z.groups * halves * z.pairs, 128)
    short = shape((z.groups, halves * z.pairs, 128), BF16)
    rows_scratch = [pltpu.VMEM(rows, F32)]
    tables = jnp.asarray(dft_tables(z.freqs * z.groups, z.times))

    def over_tile(x):
        return lax.all_to_all(x, "tile", split_axis=0, concat_axis=0, tiled=True)

    def over_freq(x):
        return lax.all_to_all(x, "freq", split_axis=0, concat_axis=0, tiled=True)

    def far(x):
        return pltpu.with_memory_space_constraint(x, pltpu.HBM)

    held = [pltpu.VMEM(x.shape, x.dtype) for x in (left, recorded, tile_ranks, tile_scales)]
    held += [pltpu.SMEM(x.shape, x.dtype) for x in (step_sizes, thresholds)]
    held += [pltpu.SemaphoreType.DMA((z.freqs, z.rows, 4)), pltpu.SemaphoreType.DMA((5,))]
    duals, row_weight, col_weight, scalars = run(
        "first_duals", part(first_duals_kernel, z), [HBM] * 6, [coefs, weights, weights, shape((8, 128), F32)], held
    )(far(left), far(recorded), far(tile_ranks), far(tile_scales), far(step_sizes), far(thresholds))
    update = run("first_gradient", part(first_gradient_kernel, z), [VMEM] * 3, shape(rows, F32))(
        right, over_tile(duals), scalars
    )
    sent, first = run(
        "first_threshold", part(first_threshold_kernel, z), [VMEM] * 3, [short, shape((z.times, z.side), F32)]
    )(over_freq(update.reshape(z.groups, halves * z.pairs, 128)), tables, scalars)
    coeffs = run("coefficients", part(coefficients_kernel, z), [VMEM] * 3, coefs, rows_scratch)(
        right, over_freq(sent), col_weight
    )
    duals = run("residual", part(residual_kernel, z), [VMEM] * 4, coefs)(
        left, over_tile(coeffs), recorded, row_weight
    )
    update = run("second_gradient", part(second_gradient_kernel, z), [VMEM] * 3, short, rows_scratch)(
        right, over_tile(duals), scalars
    )
    sent = run("second_threshold", part(second_threshold_kernel, z), [VMEM] * 4, short)(
        over_freq(update), first, tables, scalars
    )
    out = shape((z.freqs, 2, z.virtual, z.cols * z.side), F32)
    return run("output", part(output_kernel, z), [VMEM], out, rows_scratch)(over_freq(sent))


def solution(mesh):
    return jax.shard_map(
        functools.partial(per_device, tiles=mesh.shape["tile"], groups=mesh.shape["freq"]),
        mesh=mesh,
        in_specs=(
            P("freq", "tile", None, None, None, None),
            P("freq", None, "tile", None, None, None),
            P("freq", None, None),
            P("freq", None, None, None),
            P("freq", None, None, "tile"),
            P("freq"),
            P(),
        ),
        out_specs=P("freq", None, None, "tile"),
        check_vma=False,
    )
```

time: 121 us -> 105 us (0.87)
  Pallas kernels: 18.6 us -> 12.4 us
  local copies, waits for them, and re-layouts: 5.06 us -> 0.02 us
  blocking collectives: 96.4 us -> 92 us
    pallas_call x8, Pallas kernels: 18.6 us -> 12.4 us  [the longest x1 4.53 us: per_device(): run('first_duals', part(first_duals_kernel, z), [HBM] * 6, [coefs, weight...]
    unnamed x24 -> x8, local copies, waits for them, and re-layouts: 5.06 us -> 0.02 us
    all_to_all x4, blocking collectives: 58.3 us -> 54.3 us  [over_freq(): return lax.all_to_all(x, 'freq', split_axis=0, concat_axis=0, tiled=True)]
where the time goes in v2:
time: 105 us
  blocking collectives  92 us (88%)
  Pallas kernels  12.4 us (12%)
    all_to_all x4, blocking collectives, over_freq(): return lax.all_to_all(x, 'freq', split_axis=0, concat_axis=0, tiled=True)  54.3 us
    all_to_all x3, blocking collectives, over_tile(): return lax.all_to_all(x, 'tile', split_axis=0, concat_axis=0, tiled=True)  37.7 us
    pallas_call x1, Pallas kernels, per_device(): run('first_duals', part(first_duals_kernel, z), [HBM] * 6, [coefs, weight...  4.53 us
    pallas_call x1, Pallas kernels, per_device(): run('residual', part(residual_kernel, z), [VMEM] * 4, coefs)  2.36 us

profile of v2, /device:TPU:1, one launch (start us, length us, event | category | flops | bytes accessed | tf_op | source)
XLA Modules:
  0.0 104.5 jit_solution(1017369733420781251)
XLA Ops:
  0.0 0.0 copy-start
  0.0 0.0 copy-start.2
  0.0 4.5 %first_duals.1 = (bf16[8,4,16,128]{3,2,1,0:T(8,128)(2,1)S(1)}, f32[32,128]{1,0:T(8,128)S(1)}, f32[32,128]{1,0:T(8,128)S(1)}, f32[8,128]{1,0:T(8,128)S(1)}) custom-call(bf16[4,2,32,2,16,256]{5,4,3,2,1,0:T(8,128)(2,1)} %left.1, f32[4,2,8,512]{3,2,1,0:T(8,128)} %recorded_ref.1, s32[4,16,32]{2,1,0:T(8,128)} %ranks_hbm.1, f32[4,2,16,32]{3,2,1,0:T(8,128)} %scales_hbm.1, ...), custom_call_target="tpu_custom_call" | custom-call | tf_op jit(solution)/shard_map/first_duals/pallas_call | solution.py:343
  4.5 16.6 %all_to_all.35.arrived_ref = bf16[8,4,16,128]{3,2,1,0:T(8,128)(2,1)S(1)} all-to-all(bf16[8,4,16,128]{3,2,1,0:T(8,128)(2,1)S(1)} %get-tuple-element.11), channel_id=1, replica_groups=mesh['freq'=32,'tile'=8] {'tile'}, dimensions={0} | all-to-all | bytes 262144 | tf_op jit(solution)/shard_map/all_to_all | solution.py:332
  21.1 0.0 copy-done
  21.1 1.0 first_gradient.1
  22.1 0.0 copy-start.1
  22.1 0.0 copy-start.3
  22.1 18.3 %all_to_all.36.arrived_ref = f32[32,16,128]{2,1,0:T(8,128)S(1)} all-to-all(f32[32,16,128]{2,1,0:T(8,128)S(1)} %bitcast.1), channel_id=1, replica_groups=mesh['freq'=32,'tile'=8] {'freq'}, dimensions={0} | all-to-all | bytes 524288 | tf_op jit(solution)/shard_map/all_to_all | solution.py:335
  40.5 0.0 copy-done.2
  40.5 0.7 first_threshold.1
  41.1 11.2 %all_to_all.37.field_ref = bf16[32,16,128]{2,1,0:T(8,128)(2,1)S(1)} all-to-all(bf16[32,16,128]{2,1,0:T(8,128)(2,1)S(1)} %get-tuple-element.13), channel_id=1, replica_groups=mesh['freq'=32,'tile'=8] {'freq'}, dimensions={0} | all-to-all | bytes 262144 | tf_op jit(solution)/shard_map/all_to_all | solution.py:335
  52.3 1.4 %coefficients.1 = bf16[8,4,16,128]{3,2,1,0:T(8,128)(2,1)S(1)} custom-call(bf16[4,16,4,2,16,256]{5,4,3,2,1,0:T(8,128)(2,1)S(1)} %copy-done, bf16[32,16,128]{2,1,0:T(8,128)(2,1)S(1)} %all_to_all.37.field_ref, f32[32,128]{1,0:T(8,128)S(1)} %get-tuple-element.14.weights_ref), custom_call_target="tpu_custom_call" | custom-call | tf_op jit(solution)/shard_map/coefficients/pallas_call | solution.py:352
  53.7 10.8 %all_to_all.38.arrived_ref = bf16[8,4,16,128]{3,2,1,0:T(8,128)(2,1)S(1)} all-to-all(bf16[8,4,16,128]{3,2,1,0:T(8,128)(2,1)S(1)} %coefficients.1), channel_id=1, replica_groups=mesh['freq'=32,'tile'=8] {'tile'}, dimensions={0} | all-to-all | bytes 262144 | tf_op jit(solution)/shard_map/all_to_all | solution.py:332
  64.5 0.0 copy-done.1
  64.5 0.0 copy-done.3
  64.5 2.4 %residual.1 = bf16[8,4,16,128]{3,2,1,0:T(8,128)(2,1)S(1)} custom-call(bf16[4,2,32,2,16,256]{5,4,3,2,1,0:T(8,128)(2,1)S(1)} %copy-done.1, bf16[8,4,16,128]{3,2,1,0:T(8,128)(2,1)S(1)} %all_to_all.38.arrived_ref, f32[4,2,8,512]{3,2,1,0:T(8,128)S(1)} %copy-done.3, f32[32,128]{1,0:T(8,128)S(1)} %get-tuple-element.15.weights_ref), custom_call_target="tpu_custom_call" | custom-call | tf_op jit(solution)/shard_map/residual/pallas_call | solution.py:355
  66.8 10.3 %all_to_all.39.arrived_ref = bf16[8,4,16,128]{3,2,1,0:T(8,128)(2,1)S(1)} all-to-all(bf16[8,4,16,128]{3,2,1,0:T(8,128)(2,1)S(1)} %residual.1), channel_id=1, replica_groups=mesh['freq'=32,'tile'=8] {'tile'}, dimensions={0} | all-to-all | bytes 262144 | tf_op jit(solution)/shard_map/all_to_all | solution.py:332
  77.2 1.0 second_gradient.1
  78.2 13.5 %all_to_all.40.arrived_ref = bf16[32,16,128]{2,1,0:T(8,128)(2,1)S(1)} all-to-all(bf16[32,16,128]{2,1,0:T(8,128)(2,1)S(1)} %second_gradient.1), channel_id=1, replica_groups=mesh['freq'=32,'tile'=8] {'freq'}, dimensions={0} | all-to-all | bytes 262144 | tf_op jit(solution)/shard_map/all_to_all | solution.py:335
  91.7 0.7 second_threshold.1
  92.4 11.3 %all_to_all.41.field_ref = bf16[32,16,128]{2,1,0:T(8,128)(2,1)S(1)} all-to-all(bf16[32,16,128]{2,1,0:T(8,128)(2,1)S(1)} %second_threshold.1), channel_id=1, replica_groups=mesh['freq'=32,'tile'=8] {'freq'}, dimensions={0} | all-to-all | bytes 262144 | tf_op jit(solution)/shard_map/all_to_all | solution.py:335
  103.7 0.9 output.1
Async XLA Ops:
  0.0 21.1 %copy-start = (bf16[4,16,4,2,16,256]{5,4,3,2,1,0:T(8,128)(2,1)S(1)}, bf16[4,16,4,2,16,256]{5,4,3,2,1,0:T(8,128)(2,1)}, u32[]{:S(2)}) copy-start(bf16[4,16,4,2,16,256]{5,4,3,2,1,0:T(8,128)(2,1)} %right.5) | copy-start | bytes 12582916
  0.0 40.5 %copy-start.2 = (bf16[2,256,768]{2,1,0:T(8,128)(2,1)S(1)}, bf16[2,256,768]{2,1,0:T(8,128)(2,1)}, u32[]{:S(2)}) copy-start(bf16[2,256,768]{2,1,0:T(8,128)(2,1)} %constant.2.clone.tables_ref) | copy-start | bytes 2359300
  22.1 42.4 %copy-start.1 = (bf16[4,2,32,2,16,256]{5,4,3,2,1,0:T(8,128)(2,1)S(1)}, bf16[4,2,32,2,16,256]{5,4,3,2,1,0:T(8,128)(2,1)}, u32[]{:S(2)}) copy-start(bf16[4,2,32,2,16,256]{5,4,3,2,1,0:T(8,128)(2,1)} %left.1) | copy-start | bytes 12582916
  22.1 42.4 %copy-start.3 = (f32[4,2,8,512]{3,2,1,0:T(8,128)S(1)}, f32[4,2,8,512]{3,2,1,0:T(8,128)}, u32[]{:S(2)}) copy-start(f32[4,2,8,512]{3,2,1,0:T(8,128)} %recorded_ref.1) | copy-start | bytes 393220

commit v3 on v2

--- a/solution.py
+++ b/solution.py
@@ -50,10 +50,16 @@
 
 
 def expand_weights(z, scales, ranks, expand):
-    wide = jnp.dot(scales, expand, precision=HIGHEST, preferred_element_type=F32)
-    live = jnp.dot(ranks.astype(BF16), expand.astype(BF16), preferred_element_type=F32)
-    slot = (lax.broadcasted_iota(jnp.int32, wide.shape, 1) % z.slots).astype(F32)
-    return jnp.where(slot < live, wide, 0.0)
+    terms, rest = [], scales
+    for _ in range(3):
+        terms.append(rest.astype(BF16).astype(F32))
+        rest = rest - terms[-1]
+    zero = jnp.zeros_like(ranks)
+    left = jnp.concatenate([jnp.concatenate(terms, 1), jnp.concatenate([ranks, zero, zero], 1)], 0)
+    wide = jnp.dot(left.astype(BF16), jnp.concatenate([expand] * 3, 0).astype(BF16), preferred_element_type=F32)
+    count = scales.shape[0]
+    slot = (lax.broadcasted_iota(jnp.int32, (count, z.lanes), 1) % z.slots).astype(F32)
+    return jnp.where(slot < wide[count:], wide[:count], 0.0)
 
 
 def row_weights(z, here, ranks_ref, scales_ref):
@@ -155,38 +161,28 @@
             )
         )
     ]
-    wide = z.col_tiles // 4
-    copies = [
-        [
-            pltpu.make_async_copy(
-                left_hbm.at[f, r, pl.ds(q * wide, wide)], u.at[f, r, pl.ds(q * wide, wide)], sems.at[f, r, q]
-            )
-            for r in range(z.rows)
-            for q in range(4)
-        ]
-        for f in range(z.freqs)
-    ]
-    for copy in little + [copy for group in copies for copy in group]:
+    copies = [pltpu.make_async_copy(left_hbm.at[f], u.at[f], sems.at[f]) for f in range(z.freqs)]
+    for copy in little + copies:
         copy.start()
     little[0].wait()
     little[1].wait()
     row_ref[...] = row_weights(z, here, ranks, scales)
     col_ref[...] = column_weights(z, here, ranks, scales)
-    for copy in little[2:]:
-        copy.wait()
-    at = lax.broadcasted_iota(jnp.int32, scalars_ref.shape, 0)
-    scalars = jnp.full(scalars_ref.shape, levels[lax.axis_index("freq") // z.cols], F32)
-    for f in range(z.freqs):
-        scalars = jnp.where(at == f, steps[f], scalars)
-    scalars_ref[...] = scalars
+    little[2].wait()
     for f in range(z.freqs):
         vectors = []
         for r in range(z.rows):
             at = slice(r * z.side, (r + 1) * z.side)
             vectors.append((recorded[f, 0, :, at], recorded[f, 1, :, at]))
-        for copy in copies[f]:
-            copy.wait()
+        copies[f].wait()
         contract(z, left_block, u, f, vectors, 0, row_ref, out_ref)
+    little[3].wait()
+    little[4].wait()
+    at = lax.broadcasted_iota(jnp.int32, scalars_ref.shape, 0)
+    scalars = jnp.full(scalars_ref.shape, levels[lax.axis_index("freq") // z.cols], F32)
+    for f in range(z.freqs):
+        scalars = jnp.where(at == f, steps[f], scalars)
+    scalars_ref[...] = scalars
 
 
 def source_rows(z, f, c, j, half):
@@ -261,8 +257,8 @@
 
 def residual_kernel(z, left, arrived_ref, recorded_ref, weights_ref, out_ref):
     v = z.virtual
-    for f in range(z.freqs):
-        image = combine(z, left_block, left, f, arrived_ref, 0, z.rows)
+    images = [combine(z, left_block, left, f, arrived_ref, 0, z.rows) for f in range(z.freqs)]
+    for f, image in enumerate(images):
         vectors = []
         for r in range(z.rows):
             at = slice(r * z.side, (r + 1) * z.side)
@@ -276,12 +272,17 @@
         contract(z, left_block, left, f, vectors, 0, weights_ref, out_ref)
 
 
-def output_kernel(z, field_ref, out_ref, rows_ref):
+def output_kernel(z, field_ref, out_hbm, rows_ref, held, sems):
     rows_ref[...] = field_ref[...].astype(F32).reshape(rows_ref.shape)
+    copies = []
     for f in range(z.freqs):
         for c in range(2):
             for j in range(z.cols):
-                out_ref[f, c, :, j * z.side : (j + 1) * z.side] = field_rows(z, rows_ref, f, c, j)
+                held[f, c, :, j * z.side : (j + 1) * z.side] = field_rows(z, rows_ref, f, c, j)
+        copies.append(pltpu.make_async_copy(held.at[f], out_hbm.at[f], sems.at[f]))
+        copies[f].start()
+    for copy in copies:
+        copy.wait()
 
 
 def dft_tables(freqs, times):
@@ -303,15 +304,16 @@
 VMEM = pl.BlockSpec(memory_space=pltpu.VMEM)
 
 
-def run(name, kernel, in_specs, out, scratch=()):
+def run(name, kernel, in_specs, out, scratch=(), out_specs=VMEM, cost=None):
     return pl.pallas_call(
         kernel,
         name=name,
         in_specs=in_specs,
-        out_specs=VMEM if isinstance(out, jax.ShapeDtypeStruct) else [VMEM] * len(out),
+        out_specs=out_specs if isinstance(out, jax.ShapeDtypeStruct) else [out_specs] * len(out),
         out_shape=out,
         scratch_shapes=list(scratch),
         interpret=INTERPRET,
+        cost_estimate=cost,
         compiler_params=pltpu.CompilerParams(vmem_limit_bytes=40 << 20),
     )
 
@@ -339,7 +341,7 @@
 
     held = [pltpu.VMEM(x.shape, x.dtype) for x in (left, recorded, tile_ranks, tile_scales)]
     held += [pltpu.SMEM(x.shape, x.dtype) for x in (step_sizes, thresholds)]
-    held += [pltpu.SemaphoreType.DMA((z.freqs, z.rows, 4)), pltpu.SemaphoreType.DMA((5,))]
+    held += [pltpu.SemaphoreType.DMA((z.freqs,)), pltpu.SemaphoreType.DMA((5,))]
     duals, row_weight, col_weight, scalars = run(
         "first_duals", part(first_duals_kernel, z), [HBM] * 6, [coefs, weights, weights, shape((8, 128), F32)], held
     )(far(left), far(recorded), far(tile_ranks), far(tile_scales), far(step_sizes), far(thresholds))
@@ -362,7 +364,8 @@
         over_freq(update), first, tables, scalars
     )
     out = shape((z.freqs, 2, z.virtual, z.cols * z.side), F32)
-    return run("output", part(output_kernel, z), [VMEM], out, rows_scratch)(over_freq(sent))
+    held = rows_scratch + [pltpu.VMEM(out.shape, F32), pltpu.SemaphoreType.DMA((z.freqs,))]
+    return run("output", part(output_kernel, z), [VMEM], out, held, HBM)(over_freq(sent))
 
 
 def solution(mesh):

time: 105 us -> 103 us (0.981)
  Pallas kernels: 12.4 us -> 10.8 us
    pallas_call x1, Pallas kernels: 4.53 us -> 3.22 us  [per_device(): run('first_duals', part(first_duals_kernel, z), [HBM] * 6, [coefs, weight...]
where the time goes in v3:
time: 103 us
  blocking collectives  92 us (89%)
  Pallas kernels  10.8 us (10%)
    all_to_all x4, blocking collectives, over_freq(): return lax.all_to_all(x, 'freq', split_axis=0, concat_axis=0, tiled=True)  54.3 us
    all_to_all x3, blocking collectives, over_tile(): return lax.all_to_all(x, 'tile', split_axis=0, concat_axis=0, tiled=True)  37.7 us
    pallas_call x1, Pallas kernels, per_device(): run('first_duals', part(first_duals_kernel, z), [HBM] * 6, [coefs, weight...  3.22 us

profile of v3, /device:TPU:1, one launch (start us, length us, event | category | flops | bytes accessed | tf_op | source)
XLA Modules:
  0.0 102.8 jit_solution(12302457742204561944)
XLA Ops:
  0.0 0.0 copy-start
  0.0 0.0 copy-start.2
  0.0 3.2 %first_duals.1 = (bf16[8,4,16,128]{3,2,1,0:T(8,128)(2,1)S(1)}, f32[32,128]{1,0:T(8,128)S(1)}, f32[32,128]{1,0:T(8,128)S(1)}, f32[8,128]{1,0:T(8,128)S(1)}) custom-call(bf16[4,2,32,2,16,256]{5,4,3,2,1,0:T(8,128)(2,1)} %left.1, f32[4,2,8,512]{3,2,1,0:T(8,128)} %recorded_ref.1, s32[4,16,32]{2,1,0:T(8,128)} %ranks_hbm.1, f32[4,2,16,32]{3,2,1,0:T(8,128)} %scales_hbm.1, ...), custom_call_target="tpu_custom_call" | custom-call | tf_op jit(solution)/shard_map/first_duals/pallas_call | solution.py:345
  3.2 16.6 %all_to_all.35.arrived_ref = bf16[8,4,16,128]{3,2,1,0:T(8,128)(2,1)S(1)} all-to-all(bf16[8,4,16,128]{3,2,1,0:T(8,128)(2,1)S(1)} %get-tuple-element.11), channel_id=1, replica_groups=mesh['freq'=32,'tile'=8] {'tile'}, dimensions={0} | all-to-all | bytes 262144 | tf_op jit(solution)/shard_map/all_to_all | solution.py:334
  19.8 0.0 copy-done
  19.8 1.0 first_gradient.1
  20.8 0.0 copy-start.1
  20.8 0.0 copy-start.3
  20.8 18.3 %all_to_all.36.arrived_ref = f32[32,16,128]{2,1,0:T(8,128)S(1)} all-to-all(f32[32,16,128]{2,1,0:T(8,128)S(1)} %bitcast.1), channel_id=1, replica_groups=mesh['freq'=32,'tile'=8] {'freq'}, dimensions={0} | all-to-all | bytes 524288 | tf_op jit(solution)/shard_map/all_to_all | solution.py:337
  39.1 0.0 copy-done.2
  39.2 0.7 first_threshold.1
  39.8 11.2 %all_to_all.37.field_ref = bf16[32,16,128]{2,1,0:T(8,128)(2,1)S(1)} all-to-all(bf16[32,16,128]{2,1,0:T(8,128)(2,1)S(1)} %get-tuple-element.13), channel_id=1, replica_groups=mesh['freq'=32,'tile'=8] {'freq'}, dimensions={0} | all-to-all | bytes 262144 | tf_op jit(solution)/shard_map/all_to_all | solution.py:337
  51.0 1.4 %coefficients.1 = bf16[8,4,16,128]{3,2,1,0:T(8,128)(2,1)S(1)} custom-call(bf16[4,16,4,2,16,256]{5,4,3,2,1,0:T(8,128)(2,1)S(1)} %copy-done, bf16[32,16,128]{2,1,0:T(8,128)(2,1)S(1)} %all_to_all.37.field_ref, f32[32,128]{1,0:T(8,128)S(1)} %get-tuple-element.14.weights_ref), custom_call_target="tpu_custom_call" | custom-call | tf_op jit(solution)/shard_map/coefficients/pallas_call | solution.py:354
  52.4 10.8 %all_to_all.38.arrived_ref = bf16[8,4,16,128]{3,2,1,0:T(8,128)(2,1)S(1)} all-to-all(bf16[8,4,16,128]{3,2,1,0:T(8,128)(2,1)S(1)} %coefficients.1), channel_id=1, replica_groups=mesh['freq'=32,'tile'=8] {'tile'}, dimensions={0} | all-to-all | bytes 262144 | tf_op jit(solution)/shard_map/all_to_all | solution.py:334
  63.2 0.0 copy-done.1
  63.2 0.0 copy-done.3
  63.2 2.0 %residual.1 = bf16[8,4,16,128]{3,2,1,0:T(8,128)(2,1)S(1)} custom-call(bf16[4,2,32,2,16,256]{5,4,3,2,1,0:T(8,128)(2,1)S(1)} %copy-done.1, bf16[8,4,16,128]{3,2,1,0:T(8,128)(2,1)S(1)} %all_to_all.38.arrived_ref, f32[4,2,8,512]{3,2,1,0:T(8,128)S(1)} %copy-done.3, f32[32,128]{1,0:T(8,128)S(1)} %get-tuple-element.15.weights_ref), custom_call_target="tpu_custom_call" | custom-call | tf_op jit(solution)/shard_map/residual/pallas_call | solution.py:357
  65.2 10.3 %all_to_all.39.arrived_ref = bf16[8,4,16,128]{3,2,1,0:T(8,128)(2,1)S(1)} all-to-all(bf16[8,4,16,128]{3,2,1,0:T(8,128)(2,1)S(1)} %residual.1), channel_id=1, replica_groups=mesh['freq'=32,'tile'=8] {'tile'}, dimensions={0} | all-to-all | bytes 262144 | tf_op jit(solution)/shard_map/all_to_all | solution.py:334
  75.5 1.0 second_gradient.1
  76.5 13.5 %all_to_all.40.arrived_ref = bf16[32,16,128]{2,1,0:T(8,128)(2,1)S(1)} all-to-all(bf16[32,16,128]{2,1,0:T(8,128)(2,1)S(1)} %second_gradient.1), channel_id=1, replica_groups=mesh['freq'=32,'tile'=8] {'freq'}, dimensions={0} | all-to-all | bytes 262144 | tf_op jit(solution)/shard_map/all_to_all | solution.py:337
  90.1 0.7 second_threshold.1
  90.7 11.3 %all_to_all.41.field_ref = bf16[32,16,128]{2,1,0:T(8,128)(2,1)S(1)} all-to-all(bf16[32,16,128]{2,1,0:T(8,128)(2,1)S(1)} %second_threshold.1), channel_id=1, replica_groups=mesh['freq'=32,'tile'=8] {'freq'}, dimensions={0} | all-to-all | bytes 262144 | tf_op jit(solution)/shard_map/all_to_all | solution.py:337
  102.0 0.8 output.1
Async XLA Ops:
  0.0 19.8 %copy-start = (bf16[4,16,4,2,16,256]{5,4,3,2,1,0:T(8,128)(2,1)S(1)}, bf16[4,16,4,2,16,256]{5,4,3,2,1,0:T(8,128)(2,1)}, u32[]{:S(2)}) copy-start(bf16[4,16,4,2,16,256]{5,4,3,2,1,0:T(8,128)(2,1)} %right.5) | copy-start | bytes 12582916
  0.0 39.1 %copy-start.2 = (bf16[2,256,768]{2,1,0:T(8,128)(2,1)S(1)}, bf16[2,256,768]{2,1,0:T(8,128)(2,1)}, u32[]{:S(2)}) copy-start(bf16[2,256,768]{2,1,0:T(8,128)(2,1)} %constant.2.clone.tables_ref) | copy-start | bytes 2359300
  20.8 42.4 %copy-start.1 = (bf16[4,2,32,2,16,256]{5,4,3,2,1,0:T(8,128)(2,1)S(1)}, bf16[4,2,32,2,16,256]{5,4,3,2,1,0:T(8,128)(2,1)}, u32[]{:S(2)}) copy-start(bf16[4,2,32,2,16,256]{5,4,3,2,1,0:T(8,128)(2,1)} %left.1) | copy-start | bytes 12582916
  20.8 42.4 %copy-start.3 = (f32[4,2,8,512]{3,2,1,0:T(8,128)S(1)}, f32[4,2,8,512]{3,2,1,0:T(8,128)}, u32[]{:S(2)}) copy-start(f32[4,2,8,512]{3,2,1,0:T(8,128)} %recorded_ref.1) | copy-start | bytes 393220

commit v4 on v3

--- a/solution.py
+++ b/solution.py
@@ -14,6 +14,7 @@
 BF16 = jnp.bfloat16
 HIGHEST = lax.Precision.HIGHEST
 NT = (((1,), (1,)), ((), ()))
+KNEE = 0.25
 INTERPRET = False
 
 
@@ -23,11 +24,12 @@
         self.row_tiles, self.cols = right.shape[1], right.shape[2]
         self.virtual = recorded.shape[2]
         self.tiles, self.groups = tiles, groups
+        self.team = groups // 2
         self.lanes = self.rows * self.cols * self.slots
         self.pairs = 2 * self.freqs
         self.times = 2 * self.freqs * groups
         assert self.lanes == 128 and self.virtual == 8 and self.tiles % 2 == 0
-        assert self.groups == self.virtual * self.cols and self.slots == 16
+        assert self.groups == self.virtual * self.cols and self.cols % 2 == 0 and self.slots == 16
 
 
 def lane_group(z, shape, which):
@@ -179,7 +181,7 @@
     little[3].wait()
     little[4].wait()
     at = lax.broadcasted_iota(jnp.int32, scalars_ref.shape, 0)
-    scalars = jnp.full(scalars_ref.shape, levels[lax.axis_index("freq") // z.cols], F32)
+    scalars = jnp.full(scalars_ref.shape, levels[lax.axis_index("freq") % z.team // (z.team // z.virtual)], F32)
     for f in range(z.freqs):
         scalars = jnp.where(at == f, steps[f], scalars)
     scalars_ref[...] = scalars
@@ -202,46 +204,79 @@
                 rows_ref[source_rows(z, f, c, j, half), :] = part * scalars_ref[f : f + 1, :]
 
 
-def first_gradient_kernel(z, right, arrived_ref, scalars_ref, out_ref):
-    for f in range(z.freqs):
-        gradient(z, right, f, arrived_ref, scalars_ref, out_ref)
+def encode(x):
+    w = jnp.abs(x) * (1.0 / KNEE)
+    t = w + jnp.sqrt(w * w + 1.0)
+    square = t * t
+    fifth = square * square * t * 2.0**-60
+    return jnp.where(x < 0.0, -fifth * fifth, fifth * fifth).astype(BF16)
+
+
+def decode(code):
+    z = code.astype(F32)
+    t = jnp.exp((jnp.log(jnp.abs(z)) + 120.0 * math.log(2.0)) * 0.1)
+    size = (t - 1.0 / t) * (0.5 * KNEE)
+    return jnp.where(z < 0.0, -size, size)
+
+
+def send_twice(z, blocks, out_ref):
+    for team in range(2):
+        out_ref[team * z.team : (team + 1) * z.team] = blocks
+
+
+def first_gradient_kernel(z, right, arrived_ref, scalars_ref, out_ref, rows_ref):
+    for f in range(z.freqs):
+        gradient(z, right, f, arrived_ref, scalars_ref, rows_ref)
+    send_twice(z, encode(rows_ref[...].reshape(z.team, -1, 128)), out_ref)
 
 
 def second_gradient_kernel(z, right, arrived_ref, scalars_ref, out_ref, rows_ref):
     for f in range(z.freqs):
         gradient(z, right, f, arrived_ref, scalars_ref, rows_ref)
-    out_ref[...] = rows_ref[...].reshape(out_ref.shape).astype(BF16)
-
-
-def times(tables_ref, which, x):
+    send_twice(z, rows_ref[...].reshape(z.team, -1, 128).astype(BF16), out_ref)
+
+
+def times(table, x):
     high = x.astype(BF16)
     low = (x - high.astype(F32)).astype(BF16)
-    return jnp.dot(tables_ref[which], jnp.concatenate([high, low, high], 0), preferred_element_type=F32)
-
-
-def threshold(z, field, tables_ref, scalars_ref, out_ref):
-    halves = z.side // 128
-    signal = times(tables_ref, 0, field)
-    level = jnp.concatenate([scalars_ref[z.freqs : z.freqs + 1, :]] * halves, 1)
-    back = times(tables_ref, 1, signal - jnp.clip(signal, -level, level))
-    parts = [back[:, half * 128 : (half + 1) * 128].reshape(z.groups, z.pairs, 128) for half in range(halves)]
+    return jnp.dot(table, jnp.concatenate([high, low, high], 0), preferred_element_type=F32)
+
+
+def threshold(z, field, tables_ref, scalars_ref):
+    signal = times(tables_ref[0], field)
+    level = jnp.concatenate([scalars_ref[z.freqs : z.freqs + 1, :]] * (field.shape[1] // 128), 1)
+    return signal - jnp.clip(signal, -level, level)
+
+
+def send_back(z, mine, out_ref):
+    parts = [
+        mine[:, lo : lo + 128].reshape(z.team, z.pairs, 128) for lo in range(0, mine.shape[1], 128)
+    ]
     out_ref[...] = jnp.concatenate(parts, 1).astype(BF16)
-    return back
 
 
 def field_of(z, blocks):
-    halves = z.side // 128
-    parts = [blocks[:, half * z.pairs : (half + 1) * z.pairs].reshape(z.times, 128) for half in range(halves)]
+    parts = [
+        blocks[:, lo : lo + z.pairs].reshape(z.times, 128) for lo in range(0, blocks.shape[1], z.pairs)
+    ]
     return jnp.concatenate(parts, 1)
 
 
+def team_rows(z):
+    count = z.team * z.pairs
+    return pl.ds(pl.multiple_of(lax.axis_index("freq") // z.team * count, count), count)
+
+
 def first_threshold_kernel(z, arrived_ref, tables_ref, scalars_ref, out_ref, first_ref):
-    first_ref[...] = threshold(z, field_of(z, arrived_ref[...]), tables_ref, scalars_ref, out_ref)
+    kept = threshold(z, field_of(z, decode(arrived_ref[...])), tables_ref, scalars_ref)
+    first_ref[...] = times(tables_ref[1], kept)
+    send_back(z, first_ref[team_rows(z), :], out_ref)
 
 
 def second_threshold_kernel(z, arrived_ref, first_ref, tables_ref, scalars_ref, out_ref):
     field = first_ref[...] + field_of(z, arrived_ref[...].astype(F32))
-    threshold(z, field, tables_ref, scalars_ref, out_ref)
+    kept = threshold(z, field, tables_ref, scalars_ref)
+    send_back(z, times(tables_ref[1, team_rows(z), :], kept), out_ref)
 
 
 def field_rows(z, ref, f, c, j):
@@ -326,7 +361,9 @@
     coefs = shape((z.tiles, z.freqs, 2 * z.virtual, z.lanes), BF16)
     weights = shape((z.freqs * z.tiles, z.lanes), F32)
     rows = (z.groups * halves * z.pairs, 128)
-    short = shape((z.groups, halves * z.pairs, 128), BF16)
+    forth = shape((z.groups, 2 * halves * z.pairs, 128), BF16)
+    back = shape((z.team, 2 * halves * z.pairs, 128), BF16)
+    teams = [list(range(at, at + z.team)) for at in (0, z.team)]
     rows_scratch = [pltpu.VMEM(rows, F32)]
     tables = jnp.asarray(dft_tables(z.freqs * z.groups, z.times))
 
@@ -335,6 +372,9 @@
 
     def over_freq(x):
         return lax.all_to_all(x, "freq", split_axis=0, concat_axis=0, tiled=True)
+
+    def over_team(x):
+        return lax.all_to_all(x, "freq", split_axis=0, concat_axis=0, tiled=True, axis_index_groups=teams)
 
     def far(x):
         return pltpu.with_memory_space_constraint(x, pltpu.HBM)
@@ -345,27 +385,27 @@
     duals, row_weight, col_weight, scalars = run(
         "first_duals", part(first_duals_kernel, z), [HBM] * 6, [coefs, weights, weights, shape((8, 128), F32)], held
     )(far(left), far(recorded), far(tile_ranks), far(tile_scales), far(step_sizes), far(thresholds))
-    update = run("first_gradient", part(first_gradient_kernel, z), [VMEM] * 3, shape(rows, F32))(
+    update = run("first_gradient", part(first_gradient_kernel, z), [VMEM] * 3, forth, rows_scratch)(
         right, over_tile(duals), scalars
     )
     sent, first = run(
-        "first_threshold", part(first_threshold_kernel, z), [VMEM] * 3, [short, shape((z.times, z.side), F32)]
-    )(over_freq(update.reshape(z.groups, halves * z.pairs, 128)), tables, scalars)
+        "first_threshold", part(first_threshold_kernel, z), [VMEM] * 3, [back, shape((z.times, 2 * z.side), F32)]
+    )(over_freq(update), tables, scalars)
     coeffs = run("coefficients", part(coefficients_kernel, z), [VMEM] * 3, coefs, rows_scratch)(
-        right, over_freq(sent), col_weight
+        right, over_team(sent), col_weight
     )
     duals = run("residual", part(residual_kernel, z), [VMEM] * 4, coefs)(
         left, over_tile(coeffs), recorded, row_weight
     )
-    update = run("second_gradient", part(second_gradient_kernel, z), [VMEM] * 3, short, rows_scratch)(
+    update = run("second_gradient", part(second_gradient_kernel, z), [VMEM] * 3, forth, rows_scratch)(
         right, over_tile(duals), scalars
     )
-    sent = run("second_threshold", part(second_threshold_kernel, z), [VMEM] * 4, short)(
+    sent = run("second_threshold", part(second_threshold_kernel, z), [VMEM] * 4, back)(
         over_freq(update), first, tables, scalars
     )
     out = shape((z.freqs, 2, z.virtual, z.cols * z.side), F32)
     held = rows_scratch + [pltpu.VMEM(out.shape, F32), pltpu.SemaphoreType.DMA((z.freqs,))]
-    return run("output", part(output_kernel, z), [VMEM], out, held, HBM)(over_freq(sent))
+    return run("output", part(output_kernel, z), [VMEM], out, held, HBM)(over_team(sent))
 
 
 def solution(mesh):

time: 103 us -> 101 us (0.981)
  blocking collectives: 92 us -> 89.3 us
    all_to_all x4 -> x2, blocking collectives: 54.3 us -> 34.2 us  [over_freq(): return lax.all_to_all(x, 'freq', split_axis=0, concat_axis=0, tiled=True)]
    all_to_all x0 -> x2, blocking collectives: none -> 17.6 us  [over_team(): lax.all_to_all(x, 'freq', split_axis=0, concat_axis=0, tiled=True, axis_i...]
where the time goes in v4:
time: 101 us
  blocking collectives  89.3 us (88%)
  Pallas kernels  11.3 us (11%)
    all_to_all x3, blocking collectives, over_tile(): return lax.all_to_all(x, 'tile', split_axis=0, concat_axis=0, tiled=True)  37.5 us
    all_to_all x2, blocking collectives, over_freq(): return lax.all_to_all(x, 'freq', split_axis=0, concat_axis=0, tiled=True)  34.2 us
    all_to_all x2, blocking collectives, over_team(): lax.all_to_all(x, 'freq', split_axis=0, concat_axis=0, tiled=True, axis_i...  17.6 us
    pallas_call x1, Pallas kernels, per_device(): run('first_duals', part(first_duals_kernel, z), [HBM] * 6, [coefs, weight...  3.22 us
    pallas_call x1, Pallas kernels, per_device(): run('residual', part(residual_kernel, z), [VMEM] * 4, coefs)  2.03 us

profile of v4, /device:TPU:1, one launch (start us, length us, event | category | flops | bytes accessed | tf_op | source)
XLA Modules:
  0.0 100.6 jit_solution(11264220257485337824)
XLA Ops:
  0.0 0.0 copy-start
  0.0 0.0 copy-start.2
  0.0 3.2 %first_duals.1 = (bf16[8,4,16,128]{3,2,1,0:T(8,128)(2,1)S(1)}, f32[32,128]{1,0:T(8,128)S(1)}, f32[32,128]{1,0:T(8,128)S(1)}, f32[8,128]{1,0:T(8,128)S(1)}) custom-call(bf16[4,2,32,2,16,256]{5,4,3,2,1,0:T(8,128)(2,1)} %left.1, f32[4,2,8,512]{3,2,1,0:T(8,128)} %recorded_ref.1, s32[4,16,32]{2,1,0:T(8,128)} %ranks_hbm.1, f32[4,2,16,32]{3,2,1,0:T(8,128)} %scales_hbm.1, ...), custom_call_target="tpu_custom_call" | custom-call | tf_op jit(solution)/shard_map/first_duals/pallas_call | solution.py:385
  3.2 16.6 %all_to_all.35.arrived_ref = bf16[8,4,16,128]{3,2,1,0:T(8,128)(2,1)S(1)} all-to-all(bf16[8,4,16,128]{3,2,1,0:T(8,128)(2,1)S(1)} %get-tuple-element.11), channel_id=1, replica_groups=mesh['freq'=32,'tile'=8] {'tile'}, dimensions={0} | all-to-all | bytes 262144 | tf_op jit(solution)/shard_map/all_to_all | solution.py:371
  19.8 0.0 copy-done
  19.8 1.2 %first_gradient.1 = bf16[32,32,128]{2,1,0:T(8,128)(2,1)S(1)} custom-call(bf16[4,16,4,2,16,256]{5,4,3,2,1,0:T(8,128)(2,1)S(1)} %copy-done, bf16[8,4,16,128]{3,2,1,0:T(8,128)(2,1)S(1)} %all_to_all.35.arrived_ref, f32[8,128]{1,0:T(8,128)S(1)} %get-tuple-element.12.scalars_ref), custom_call_target="tpu_custom_call" | custom-call | tf_op jit(solution)/shard_map/first_gradient/pallas_call | solution.py:388
  21.0 0.0 copy-start.1
  21.0 0.0 copy-start.3
  21.0 18.3 %all_to_all.36.arrived_ref = bf16[32,32,128]{2,1,0:T(8,128)(2,1)S(1)} all-to-all(bf16[32,32,128]{2,1,0:T(8,128)(2,1)S(1)} %first_gradient.1), channel_id=1, replica_groups=mesh['freq'=32,'tile'=8] {'freq'}, dimensions={0} | all-to-all | bytes 524288 | tf_op jit(solution)/shard_map/all_to_all | solution.py:374
  39.4 0.0 copy-done.2
  39.4 1.0 first_threshold.1
  40.4 8.8 %all_to_all.37.field_ref = bf16[16,32,128]{2,1,0:T(8,128)(2,1)S(1)} all-to-all(bf16[16,32,128]{2,1,0:T(8,128)(2,1)S(1)} %get-tuple-element.13), channel_id=1, replica_groups={{0,8,16,24,32,40,48,56,64,72,80,88,96,104,112,120},{128,136,144,152,160..., dimensions={0} | all-to-all | bytes 262144 | tf_op jit(solution)/shard_map/all_to_all | solution.py:377
  49.2 1.4 %coefficients.1 = bf16[8,4,16,128]{3,2,1,0:T(8,128)(2,1)S(1)} custom-call(bf16[4,16,4,2,16,256]{5,4,3,2,1,0:T(8,128)(2,1)S(1)} %copy-done, bf16[16,32,128]{2,1,0:T(8,128)(2,1)S(1)} %all_to_all.37.field_ref, f32[32,128]{1,0:T(8,128)S(1)} %get-tuple-element.14.weights_ref), custom_call_target="tpu_custom_call" | custom-call | tf_op jit(solution)/shard_map/coefficients/pallas_call | solution.py:394
  50.5 10.6 %all_to_all.38.arrived_ref = bf16[8,4,16,128]{3,2,1,0:T(8,128)(2,1)S(1)} all-to-all(bf16[8,4,16,128]{3,2,1,0:T(8,128)(2,1)S(1)} %coefficients.1), channel_id=1, replica_groups=mesh['freq'=32,'tile'=8] {'tile'}, dimensions={0} | all-to-all | bytes 262144 | tf_op jit(solution)/shard_map/all_to_all | solution.py:371
  61.1 0.0 copy-done.1
  61.1 0.0 copy-done.3
  61.1 2.0 %residual.1 = bf16[8,4,16,128]{3,2,1,0:T(8,128)(2,1)S(1)} custom-call(bf16[4,2,32,2,16,256]{5,4,3,2,1,0:T(8,128)(2,1)S(1)} %copy-done.1, bf16[8,4,16,128]{3,2,1,0:T(8,128)(2,1)S(1)} %all_to_all.38.arrived_ref, f32[4,2,8,512]{3,2,1,0:T(8,128)S(1)} %copy-done.3, f32[32,128]{1,0:T(8,128)S(1)} %get-tuple-element.15.weights_ref), custom_call_target="tpu_custom_call" | custom-call | tf_op jit(solution)/shard_map/residual/pallas_call | solution.py:397
  63.2 10.3 %all_to_all.39.arrived_ref = bf16[8,4,16,128]{3,2,1,0:T(8,128)(2,1)S(1)} all-to-all(bf16[8,4,16,128]{3,2,1,0:T(8,128)(2,1)S(1)} %residual.1), channel_id=1, replica_groups=mesh['freq'=32,'tile'=8] {'tile'}, dimensions={0} | all-to-all | bytes 262144 | tf_op jit(solution)/shard_map/all_to_all | solution.py:371
  73.5 1.0 second_gradient.1
  74.5 15.9 %all_to_all.40.arrived_ref = bf16[32,32,128]{2,1,0:T(8,128)(2,1)S(1)} all-to-all(bf16[32,32,128]{2,1,0:T(8,128)(2,1)S(1)} %second_gradient.1), channel_id=1, replica_groups=mesh['freq'=32,'tile'=8] {'freq'}, dimensions={0} | all-to-all | bytes 524288 | tf_op jit(solution)/shard_map/all_to_all | solution.py:374
  90.3 0.7 second_threshold.1
  91.0 8.8 %all_to_all.41.field_ref = bf16[16,32,128]{2,1,0:T(8,128)(2,1)S(1)} all-to-all(bf16[16,32,128]{2,1,0:T(8,128)(2,1)S(1)} %second_threshold.1), channel_id=1, replica_groups={{0,8,16,24,32,40,48,56,64,72,80,88,96,104,112,120},{128,136,144,152,160..., dimensions={0} | all-to-all | bytes 262144 | tf_op jit(solution)/shard_map/all_to_all | solution.py:377
  99.8 0.8 output.1
Async XLA Ops:
  0.0 19.8 %copy-start = (bf16[4,16,4,2,16,256]{5,4,3,2,1,0:T(8,128)(2,1)S(1)}, bf16[4,16,4,2,16,256]{5,4,3,2,1,0:T(8,128)(2,1)}, u32[]{:S(2)}) copy-start(bf16[4,16,4,2,16,256]{5,4,3,2,1,0:T(8,128)(2,1)} %right.5) | copy-start | bytes 12582916
  0.0 39.3 %copy-start.2 = (bf16[2,256,768]{2,1,0:T(8,128)(2,1)S(1)}, bf16[2,256,768]{2,1,0:T(8,128)(2,1)}, u32[]{:S(2)}) copy-start(bf16[2,256,768]{2,1,0:T(8,128)(2,1)} %constant.2.clone.tables_ref) | copy-start | bytes 2359300
  21.0 40.1 %copy-start.1 = (bf16[4,2,32,2,16,256]{5,4,3,2,1,0:T(8,128)(2,1)S(1)}, bf16[4,2,32,2,16,256]{5,4,3,2,1,0:T(8,128)(2,1)}, u32[]{:S(2)}) copy-start(bf16[4,2,32,2,16,256]{5,4,3,2,1,0:T(8,128)(2,1)} %left.1) | copy-start | bytes 12582916
  21.0 40.1 %copy-start.3 = (f32[4,2,8,512]{3,2,1,0:T(8,128)S(1)}, f32[4,2,8,512]{3,2,1,0:T(8,128)}, u32[]{:S(2)}) copy-start(f32[4,2,8,512]{3,2,1,0:T(8,128)} %recorded_ref.1) | copy-start | bytes 393220

commit v5 on v4

--- a/solution.py
+++ b/solution.py
@@ -190,7 +190,24 @@
 def source_rows(z, f, c, j, half):
     halves = z.side // 128
     start = (j * halves + half) * z.pairs + 2 * f + c
-    return pl.ds(start, z.virtual, stride=z.cols * halves * z.pairs)
+    return pl.ds(start, z.virtual, stride=padded(z))
+
+
+def padded(z):
+    return z.cols * (z.side // 128) * z.pairs + 8
+
+
+def spread_rows(z, blocks, rows_ref):
+    held = padded(z) - 8
+    rows = blocks.astype(F32).reshape(z.virtual * held, 128)
+    for v in range(z.virtual):
+        rows_ref[v * padded(z) : v * padded(z) + held, :] = rows[v * held : (v + 1) * held]
+
+
+def gather_rows(z, rows_ref):
+    held = padded(z) - 8
+    rows = [rows_ref[v * padded(z) : v * padded(z) + held, :] for v in range(z.virtual)]
+    return jnp.concatenate(rows, 0).reshape(z.team, -1, 128)
 
 
 def gradient(z, right, f, arrived_ref, scalars_ref, rows_ref):
@@ -227,13 +244,13 @@
 def first_gradient_kernel(z, right, arrived_ref, scalars_ref, out_ref, rows_ref):
     for f in range(z.freqs):
         gradient(z, right, f, arrived_ref, scalars_ref, rows_ref)
-    send_twice(z, encode(rows_ref[...].reshape(z.team, -1, 128)), out_ref)
+    send_twice(z, encode(gather_rows(z, rows_ref)), out_ref)
 
 
 def second_gradient_kernel(z, right, arrived_ref, scalars_ref, out_ref, rows_ref):
     for f in range(z.freqs):
         gradient(z, right, f, arrived_ref, scalars_ref, rows_ref)
-    send_twice(z, rows_ref[...].reshape(z.team, -1, 128).astype(BF16), out_ref)
+    send_twice(z, gather_rows(z, rows_ref).astype(BF16), out_ref)
 
 
 def times(table, x):
@@ -284,7 +301,7 @@
 
 
 def coefficients_kernel(z, right, field_ref, weights_ref, out_ref, rows_ref):
-    rows_ref[...] = field_ref[...].astype(F32).reshape(rows_ref.shape)
+    spread_rows(z, field_ref[...], rows_ref)
     for f in range(z.freqs):
         vectors = [(field_rows(z, rows_ref, f, 0, j), field_rows(z, rows_ref, f, 1, j)) for j in range(z.cols)]
         contract(z, right_block, right, f, vectors, 1, weights_ref, out_ref)
@@ -308,7 +325,7 @@
 
 
 def output_kernel(z, field_ref, out_hbm, rows_ref, held, sems):
-    rows_ref[...] = field_ref[...].astype(F32).reshape(rows_ref.shape)
+    spread_rows(z, field_ref[...], rows_ref)
     copies = []
     for f in range(z.freqs):
         for c in range(2):
@@ -360,7 +377,7 @@
     halves = z.side // 128
     coefs = shape((z.tiles, z.freqs, 2 * z.virtual, z.lanes), BF16)
     weights = shape((z.freqs * z.tiles, z.lanes), F32)
-    rows = (z.groups * halves * z.pairs, 128)
+    rows = (z.virtual * padded(z), 128)
     forth = shape((z.groups, 2 * halves * z.pairs, 128), BF16)
     back = shape((z.team, 2 * halves * z.pairs, 128), BF16)
     teams = [list(range(at, at + z.team)) for at in (0, z.team)]

time: 101 us -> 101 us (level)
  no operation moved by 1% of the time
where the time goes in v5:
time: 101 us; the launch traced here: 100 us
  blocking collectives  89.3 us (88%)
  Pallas kernels  11 us (11%)
    all_to_all x3, blocking collectives, over_tile(): return lax.all_to_all(x, 'tile', split_axis=0, concat_axis=0, tiled=True)  37.5 us
    all_to_all x2, blocking collectives, over_freq(): return lax.all_to_all(x, 'freq', split_axis=0, concat_axis=0, tiled=True)  34.2 us
    all_to_all x2, blocking collectives, over_team(): lax.all_to_all(x, 'freq', split_axis=0, concat_axis=0, tiled=True, axis_i...  17.6 us
    pallas_call x1, Pallas kernels, per_device(): run('first_duals', part(first_duals_kernel, z), [HBM] * 6, [coefs, weight...  3.22 us
    pallas_call x1, Pallas kernels, per_device(): run('residual', part(residual_kernel, z), [VMEM] * 4, coefs)  2.02 us

profile of v5, /device:TPU:1, one launch (start us, length us, event | category | flops | bytes accessed | tf_op | source)
XLA Modules:
  0.0 100.3 jit_solution(9864904132150717352)
XLA Ops:
  0.0 0.0 copy-start
  0.0 0.0 copy-start.2
  0.0 3.2 %first_duals.1 = (bf16[8,4,16,128]{3,2,1,0:T(8,128)(2,1)S(1)}, f32[32,128]{1,0:T(8,128)S(1)}, f32[32,128]{1,0:T(8,128)S(1)}, f32[8,128]{1,0:T(8,128)S(1)}) custom-call(bf16[4,2,32,2,16,256]{5,4,3,2,1,0:T(8,128)(2,1)} %left.1, f32[4,2,8,512]{3,2,1,0:T(8,128)} %recorded_ref.1, s32[4,16,32]{2,1,0:T(8,128)} %ranks_hbm.1, f32[4,2,16,32]{3,2,1,0:T(8,128)} %scales_hbm.1, ...), custom_call_target="tpu_custom_call" | custom-call | tf_op jit(solution)/shard_map/first_duals/pallas_call | solution.py:402
  3.2 16.6 %all_to_all.35.arrived_ref = bf16[8,4,16,128]{3,2,1,0:T(8,128)(2,1)S(1)} all-to-all(bf16[8,4,16,128]{3,2,1,0:T(8,128)(2,1)S(1)} %get-tuple-element.11), channel_id=1, replica_groups=mesh['freq'=32,'tile'=8] {'tile'}, dimensions={0} | all-to-all | bytes 262144 | tf_op jit(solution)/shard_map/all_to_all | solution.py:388
  19.8 0.0 copy-done
  19.8 1.1 %first_gradient.1 = bf16[32,32,128]{2,1,0:T(8,128)(2,1)S(1)} custom-call(bf16[4,16,4,2,16,256]{5,4,3,2,1,0:T(8,128)(2,1)S(1)} %copy-done, bf16[8,4,16,128]{3,2,1,0:T(8,128)(2,1)S(1)} %all_to_all.35.arrived_ref, f32[8,128]{1,0:T(8,128)S(1)} %get-tuple-element.12.scalars_ref), custom_call_target="tpu_custom_call" | custom-call | tf_op jit(solution)/shard_map/first_gradient/pallas_call | solution.py:405
  20.9 0.0 copy-start.1
  20.9 0.0 copy-start.3
  20.9 18.3 %all_to_all.36.arrived_ref = bf16[32,32,128]{2,1,0:T(8,128)(2,1)S(1)} all-to-all(bf16[32,32,128]{2,1,0:T(8,128)(2,1)S(1)} %first_gradient.1), channel_id=1, replica_groups=mesh['freq'=32,'tile'=8] {'freq'}, dimensions={0} | all-to-all | bytes 524288 | tf_op jit(solution)/shard_map/all_to_all | solution.py:391
  39.2 0.0 copy-done.2
  39.2 1.0 first_threshold.1
  40.3 8.8 %all_to_all.37.field_ref = bf16[16,32,128]{2,1,0:T(8,128)(2,1)S(1)} all-to-all(bf16[16,32,128]{2,1,0:T(8,128)(2,1)S(1)} %get-tuple-element.13), channel_id=1, replica_groups={{0,8,16,24,32,40,48,56,64,72,80,88,96,104,112,120},{128,136,144,152,160..., dimensions={0} | all-to-all | bytes 262144 | tf_op jit(solution)/shard_map/all_to_all | solution.py:394
  49.1 1.4 %coefficients.1 = bf16[8,4,16,128]{3,2,1,0:T(8,128)(2,1)S(1)} custom-call(bf16[4,16,4,2,16,256]{5,4,3,2,1,0:T(8,128)(2,1)S(1)} %copy-done, bf16[16,32,128]{2,1,0:T(8,128)(2,1)S(1)} %all_to_all.37.field_ref, f32[32,128]{1,0:T(8,128)S(1)} %get-tuple-element.14.weights_ref), custom_call_target="tpu_custom_call" | custom-call | tf_op jit(solution)/shard_map/coefficients/pallas_call | solution.py:411
  50.4 10.6 %all_to_all.38.arrived_ref = bf16[8,4,16,128]{3,2,1,0:T(8,128)(2,1)S(1)} all-to-all(bf16[8,4,16,128]{3,2,1,0:T(8,128)(2,1)S(1)} %coefficients.1), channel_id=1, replica_groups=mesh['freq'=32,'tile'=8] {'tile'}, dimensions={0} | all-to-all | bytes 262144 | tf_op jit(solution)/shard_map/all_to_all | solution.py:388
  61.0 0.0 copy-done.1
  61.0 0.0 copy-done.3
  61.0 2.0 %residual.1 = bf16[8,4,16,128]{3,2,1,0:T(8,128)(2,1)S(1)} custom-call(bf16[4,2,32,2,16,256]{5,4,3,2,1,0:T(8,128)(2,1)S(1)} %copy-done.1, bf16[8,4,16,128]{3,2,1,0:T(8,128)(2,1)S(1)} %all_to_all.38.arrived_ref, f32[4,2,8,512]{3,2,1,0:T(8,128)S(1)} %copy-done.3, f32[32,128]{1,0:T(8,128)S(1)} %get-tuple-element.15.weights_ref), custom_call_target="tpu_custom_call" | custom-call | tf_op jit(solution)/shard_map/residual/pallas_call | solution.py:414
  63.0 10.3 %all_to_all.39.arrived_ref = bf16[8,4,16,128]{3,2,1,0:T(8,128)(2,1)S(1)} all-to-all(bf16[8,4,16,128]{3,2,1,0:T(8,128)(2,1)S(1)} %residual.1), channel_id=1, replica_groups=mesh['freq'=32,'tile'=8] {'tile'}, dimensions={0} | all-to-all | bytes 262144 | tf_op jit(solution)/shard_map/all_to_all | solution.py:388
  73.4 0.9 second_gradient.1
  74.3 15.9 %all_to_all.40.arrived_ref = bf16[32,32,128]{2,1,0:T(8,128)(2,1)S(1)} all-to-all(bf16[32,32,128]{2,1,0:T(8,128)(2,1)S(1)} %second_gradient.1), channel_id=1, replica_groups=mesh['freq'=32,'tile'=8] {'freq'}, dimensions={0} | all-to-all | bytes 524288 | tf_op jit(solution)/shard_map/all_to_all | solution.py:391
  90.1 0.7 second_threshold.1
  90.8 8.8 %all_to_all.41.field_ref = bf16[16,32,128]{2,1,0:T(8,128)(2,1)S(1)} all-to-all(bf16[16,32,128]{2,1,0:T(8,128)(2,1)S(1)} %second_threshold.1), channel_id=1, replica_groups={{0,8,16,24,32,40,48,56,64,72,80,88,96,104,112,120},{128,136,144,152,160..., dimensions={0} | all-to-all | bytes 262144 | tf_op jit(solution)/shard_map/all_to_all | solution.py:394
  99.6 0.8 output.1
Async XLA Ops:
  0.0 19.8 %copy-start = (bf16[4,16,4,2,16,256]{5,4,3,2,1,0:T(8,128)(2,1)S(1)}, bf16[4,16,4,2,16,256]{5,4,3,2,1,0:T(8,128)(2,1)}, u32[]{:S(2)}) copy-start(bf16[4,16,4,2,16,256]{5,4,3,2,1,0:T(8,128)(2,1)} %right.5) | copy-start | bytes 12582916
  0.0 39.2 %copy-start.2 = (bf16[2,256,768]{2,1,0:T(8,128)(2,1)S(1)}, bf16[2,256,768]{2,1,0:T(8,128)(2,1)}, u32[]{:S(2)}) copy-start(bf16[2,256,768]{2,1,0:T(8,128)(2,1)} %constant.2.clone.tables_ref) | copy-start | bytes 2359300
  20.9 40.1 %copy-start.1 = (bf16[4,2,32,2,16,256]{5,4,3,2,1,0:T(8,128)(2,1)S(1)}, bf16[4,2,32,2,16,256]{5,4,3,2,1,0:T(8,128)(2,1)}, u32[]{:S(2)}) copy-start(bf16[4,2,32,2,16,256]{5,4,3,2,1,0:T(8,128)(2,1)} %left.1) | copy-start | bytes 12582916
  20.9 40.1 %copy-start.3 = (f32[4,2,8,512]{3,2,1,0:T(8,128)S(1)}, f32[4,2,8,512]{3,2,1,0:T(8,128)}, u32[]{:S(2)}) copy-start(f32[4,2,8,512]{3,2,1,0:T(8,128)} %recorded_ref.1) | copy-start | bytes 393220

commit v6 on v5

--- a/solution.py
+++ b/solution.py
@@ -129,7 +129,7 @@
 
 
 def combine(z, block, ref, f, arrived_ref, which, count):
-    total = None
+    lefts, rights = [], []
     v = z.virtual
     for pair in range(z.tiles // 2):
         coefs = jnp.concatenate([arrived_ref[2 * pair, f], arrived_ref[2 * pair + 1, f]], 1).astype(F32)
@@ -139,11 +139,11 @@
         for rows in (coefs, turned):
             sides.append(jnp.concatenate([jnp.where(group == at, rows, 0.0) for at in range(count)], 0))
         parts = [block_pair(block, z, ref, f, c, pair) for c in range(2)]
-        part = jnp.dot(
-            jnp.concatenate(sides, 1).astype(BF16), jnp.concatenate(parts, 0), preferred_element_type=F32
-        )
-        total = part if total is None else total + part
-    return total
+        lefts += sides
+        rights += parts
+    return jnp.dot(
+        jnp.concatenate(lefts, 1).astype(BF16), jnp.concatenate(rights, 0), preferred_element_type=F32
+    )
 
 
 def first_duals_kernel(
@@ -231,8 +231,8 @@
 
 def decode(code):
     z = code.astype(F32)
-    t = jnp.exp((jnp.log(jnp.abs(z)) + 120.0 * math.log(2.0)) * 0.1)
-    size = (t - 1.0 / t) * (0.5 * KNEE)
+    angle = (jnp.log(jnp.abs(z)) + 120.0 * math.log(2.0)) * 0.1
+    size = (jnp.exp(angle) - jnp.exp(-angle)) * (0.5 * KNEE)
     return jnp.where(z < 0.0, -size, size)
 
 
@@ -286,7 +286,7 @@
 
 def first_threshold_kernel(z, arrived_ref, tables_ref, scalars_ref, out_ref, first_ref):
     kept = threshold(z, field_of(z, decode(arrived_ref[...])), tables_ref, scalars_ref)
-    first_ref[...] = times(tables_ref[1], kept)
+    first_ref[...] = times(tables_ref[1], kept).astype(first_ref.dtype)
     send_back(z, first_ref[team_rows(z), :], out_ref)
 
 

time: 101 us -> 101 us (level)
  no operation moved by 1% of the time
where the time goes in v6:
time: 101 us; the launch traced here: 100 us
  blocking collectives  89.3 us (88%)
  Pallas kernels  11 us (11%)
    all_to_all x3, blocking collectives, over_tile(): return lax.all_to_all(x, 'tile', split_axis=0, concat_axis=0, tiled=True)  37.5 us
    all_to_all x2, blocking collectives, over_freq(): return lax.all_to_all(x, 'freq', split_axis=0, concat_axis=0, tiled=True)  34.2 us
    all_to_all x2, blocking collectives, over_team(): lax.all_to_all(x, 'freq', split_axis=0, concat_axis=0, tiled=True, axis_i...  17.6 us
    pallas_call x1, Pallas kernels, per_device(): run('first_duals', part(first_duals_kernel, z), [HBM] * 6, [coefs, weight...  3.22 us
    pallas_call x1, Pallas kernels, per_device(): run('residual', part(residual_kernel, z), [VMEM] * 4, coefs)  2.02 us

profile of v6, /device:TPU:1, one launch (start us, length us, event | category | flops | bytes accessed | tf_op | source)
XLA Modules:
  0.0 100.4 jit_solution(13034920541400442166)
XLA Ops:
  0.0 0.0 copy-start
  0.0 0.0 copy-start.2
  0.0 3.2 %first_duals.1 = (bf16[8,4,16,128]{3,2,1,0:T(8,128)(2,1)S(1)}, f32[32,128]{1,0:T(8,128)S(1)}, f32[32,128]{1,0:T(8,128)S(1)}, f32[8,128]{1,0:T(8,128)S(1)}) custom-call(bf16[4,2,32,2,16,256]{5,4,3,2,1,0:T(8,128)(2,1)} %left.1, f32[4,2,8,512]{3,2,1,0:T(8,128)} %recorded_ref.1, s32[4,16,32]{2,1,0:T(8,128)} %ranks_hbm.1, f32[4,2,16,32]{3,2,1,0:T(8,128)} %scales_hbm.1, ...), custom_call_target="tpu_custom_call" | custom-call | tf_op jit(solution)/shard_map/first_duals/pallas_call | solution.py:402
  3.2 16.6 %all_to_all.35.arrived_ref = bf16[8,4,16,128]{3,2,1,0:T(8,128)(2,1)S(1)} all-to-all(bf16[8,4,16,128]{3,2,1,0:T(8,128)(2,1)S(1)} %get-tuple-element.11), channel_id=1, replica_groups=mesh['freq'=32,'tile'=8] {'tile'}, dimensions={0} | all-to-all | bytes 262144 | tf_op jit(solution)/shard_map/all_to_all | solution.py:388
  19.8 0.0 copy-done
  19.8 1.1 %first_gradient.1 = bf16[32,32,128]{2,1,0:T(8,128)(2,1)S(1)} custom-call(bf16[4,16,4,2,16,256]{5,4,3,2,1,0:T(8,128)(2,1)S(1)} %copy-done, bf16[8,4,16,128]{3,2,1,0:T(8,128)(2,1)S(1)} %all_to_all.35.arrived_ref, f32[8,128]{1,0:T(8,128)S(1)} %get-tuple-element.12.scalars_ref), custom_call_target="tpu_custom_call" | custom-call | tf_op jit(solution)/shard_map/first_gradient/pallas_call | solution.py:405
  20.9 0.0 copy-start.1
  20.9 0.0 copy-start.3
  20.9 18.3 %all_to_all.36.arrived_ref = bf16[32,32,128]{2,1,0:T(8,128)(2,1)S(1)} all-to-all(bf16[32,32,128]{2,1,0:T(8,128)(2,1)S(1)} %first_gradient.1), channel_id=1, replica_groups=mesh['freq'=32,'tile'=8] {'freq'}, dimensions={0} | all-to-all | bytes 524288 | tf_op jit(solution)/shard_map/all_to_all | solution.py:391
  39.2 0.0 copy-done.2
  39.2 1.0 %first_threshold.1 = (bf16[16,32,128]{2,1,0:T(8,128)(2,1)S(1)}, f32[256,512]{1,0:T(8,128)S(1)}) custom-call(bf16[32,32,128]{2,1,0:T(8,128)(2,1)S(1)} %all_to_all.36.arrived_ref, bf16[2,256,768]{2,1,0:T(8,128)(2,1)S(1)} %copy-done.2, f32[8,128]{1,0:T(8,128)S(1)} %get-tuple-element.12.scalars_ref), custom_call_target="tpu_custom_call" | custom-call | tf_op jit(solution)/shard_map/first_threshold/pallas_call | solution.py:408
  40.3 8.8 %all_to_all.37.field_ref = bf16[16,32,128]{2,1,0:T(8,128)(2,1)S(1)} all-to-all(bf16[16,32,128]{2,1,0:T(8,128)(2,1)S(1)} %get-tuple-element.13), channel_id=1, replica_groups={{0,8,16,24,32,40,48,56,64,72,80,88,96,104,112,120},{128,136,144,152,160..., dimensions={0} | all-to-all | bytes 262144 | tf_op jit(solution)/shard_map/all_to_all | solution.py:394
  49.1 1.4 %coefficients.1 = bf16[8,4,16,128]{3,2,1,0:T(8,128)(2,1)S(1)} custom-call(bf16[4,16,4,2,16,256]{5,4,3,2,1,0:T(8,128)(2,1)S(1)} %copy-done, bf16[16,32,128]{2,1,0:T(8,128)(2,1)S(1)} %all_to_all.37.field_ref, f32[32,128]{1,0:T(8,128)S(1)} %get-tuple-element.14.weights_ref), custom_call_target="tpu_custom_call" | custom-call | tf_op jit(solution)/shard_map/coefficients/pallas_call | solution.py:411
  50.5 10.6 %all_to_all.38.arrived_ref = bf16[8,4,16,128]{3,2,1,0:T(8,128)(2,1)S(1)} all-to-all(bf16[8,4,16,128]{3,2,1,0:T(8,128)(2,1)S(1)} %coefficients.1), channel_id=1, replica_groups=mesh['freq'=32,'tile'=8] {'tile'}, dimensions={0} | all-to-all | bytes 262144 | tf_op jit(solution)/shard_map/all_to_all | solution.py:388
  61.0 0.0 copy-done.1
  61.0 0.0 copy-done.3
  61.0 2.0 %residual.1 = bf16[8,4,16,128]{3,2,1,0:T(8,128)(2,1)S(1)} custom-call(bf16[4,2,32,2,16,256]{5,4,3,2,1,0:T(8,128)(2,1)S(1)} %copy-done.1, bf16[8,4,16,128]{3,2,1,0:T(8,128)(2,1)S(1)} %all_to_all.38.arrived_ref, f32[4,2,8,512]{3,2,1,0:T(8,128)S(1)} %copy-done.3, f32[32,128]{1,0:T(8,128)S(1)} %get-tuple-element.15.weights_ref), custom_call_target="tpu_custom_call" | custom-call | tf_op jit(solution)/shard_map/residual/pallas_call | solution.py:414
  63.1 10.3 %all_to_all.39.arrived_ref = bf16[8,4,16,128]{3,2,1,0:T(8,128)(2,1)S(1)} all-to-all(bf16[8,4,16,128]{3,2,1,0:T(8,128)(2,1)S(1)} %residual.1), channel_id=1, replica_groups=mesh['freq'=32,'tile'=8] {'tile'}, dimensions={0} | all-to-all | bytes 262144 | tf_op jit(solution)/shard_map/all_to_all | solution.py:388
  73.4 0.9 second_gradient.1
  74.3 15.9 %all_to_all.40.arrived_ref = bf16[32,32,128]{2,1,0:T(8,128)(2,1)S(1)} all-to-all(bf16[32,32,128]{2,1,0:T(8,128)(2,1)S(1)} %second_gradient.1), channel_id=1, replica_groups=mesh['freq'=32,'tile'=8] {'freq'}, dimensions={0} | all-to-all | bytes 524288 | tf_op jit(solution)/shard_map/all_to_all | solution.py:391
  90.1 0.7 second_threshold.1
  90.8 8.8 %all_to_all.41.field_ref = bf16[16,32,128]{2,1,0:T(8,128)(2,1)S(1)} all-to-all(bf16[16,32,128]{2,1,0:T(8,128)(2,1)S(1)} %second_threshold.1), channel_id=1, replica_groups={{0,8,16,24,32,40,48,56,64,72,80,88,96,104,112,120},{128,136,144,152,160..., dimensions={0} | all-to-all | bytes 262144 | tf_op jit(solution)/shard_map/all_to_all | solution.py:394
  99.6 0.8 output.1
Async XLA Ops:
  0.0 19.8 %copy-start = (bf16[4,16,4,2,16,256]{5,4,3,2,1,0:T(8,128)(2,1)S(1)}, bf16[4,16,4,2,16,256]{5,4,3,2,1,0:T(8,128)(2,1)}, u32[]{:S(2)}) copy-start(bf16[4,16,4,2,16,256]{5,4,3,2,1,0:T(8,128)(2,1)} %right.5) | copy-start | bytes 12582916
  0.0 39.2 %copy-start.2 = (bf16[2,256,768]{2,1,0:T(8,128)(2,1)S(1)}, bf16[2,256,768]{2,1,0:T(8,128)(2,1)}, u32[]{:S(2)}) copy-start(bf16[2,256,768]{2,1,0:T(8,128)(2,1)} %constant.2.clone.tables_ref) | copy-start | bytes 2359300
  20.9 40.1 %copy-start.1 = (bf16[4,2,32,2,16,256]{5,4,3,2,1,0:T(8,128)(2,1)S(1)}, bf16[4,2,32,2,16,256]{5,4,3,2,1,0:T(8,128)(2,1)}, u32[]{:S(2)}) copy-start(bf16[4,2,32,2,16,256]{5,4,3,2,1,0:T(8,128)(2,1)} %left.1) | copy-start | bytes 12582916
  20.9 40.1 %copy-start.3 = (f32[4,2,8,512]{3,2,1,0:T(8,128)S(1)}, f32[4,2,8,512]{3,2,1,0:T(8,128)}, u32[]{:S(2)}) copy-start(f32[4,2,8,512]{3,2,1,0:T(8,128)} %recorded_ref.1) | copy-start | bytes 393220
